TPU v7x, 32 devices: a whole 2x2x4 slice. The times are simulated.
32 devices in a mesh: seq: 4 (over x, core), shard: 8 (over z, y).
Axes of the slice: x: 2, y: 2, z: 4, core: 2. Of those that a mesh axis runs over, the one named last changes fastest.
Arguments:
- inputs: bfloat16 [8, 3072, 768], P('shard', 'seq'), may hold values from -6 to 6
- teacher: bfloat16 [8, 3072, 768], P('shard', 'seq'), may hold values from -6 to 6
- seq_lengths: int32 [8, 3], P('shard'), may hold values from 0 to 3072, as said below
- w_qkv: bfloat16 [768, 2304], P('shard'), may hold values from -0.21875 to 0.21875
- q_bias: bfloat16 [768], P('shard'), may hold values from -4 to 4
- v_bias: bfloat16 [768], P('shard'), may hold values from -0.75 to 0.75
- w_out: bfloat16 [768, 768], P('shard'), may hold values from -3.5 to 3.5
- out_bias: bfloat16 [768], P('shard'), may hold values from -4 to 4
- attn_gain: bfloat16 [768], P('shard'), may hold values from 0.5 to 1.5
- attn_shift: bfloat16 [768], P('shard'), may hold values from -4 to 4
- w_up: bfloat16 [768, 3072], P('shard'), may hold values from -0.21875 to 0.21875
- up_bias: bfloat16 [3072], P('shard'), may hold values from -4 to 4
- w_down: bfloat16 [3072, 768], P('shard'), may hold values from -0.109375 to 0.109375
- down_bias: bfloat16 [768], P('shard'), may hold values from -4 to 4
- ffn_gain: bfloat16 [768], P('shard'), may hold values from 0.5 to 1.5
- ffn_shift: bfloat16 [768], P('shard'), may hold values from -4 to 4
Outputs:
- layer_out: bfloat16 [8, 3072, 768], P('shard', 'seq')
- input_grad: bfloat16 [8, 3072, 768], P('shard', 'seq')
- grad_qkv: float32 [768, 2304], P('shard')
- grad_q_bias: float32 [768], P('shard')
- grad_v_bias: float32 [768], P('shard')
- grad_out: float32 [768, 768], P('shard')
- grad_out_bias: float32 [768], P('shard')
- grad_attn_gain: float32 [768], P('shard')
- grad_attn_shift: float32 [768], P('shard')
- grad_up: float32 [768, 3072], P('shard')
- grad_up_bias: float32 [3072], P('shard')
- grad_down: float32 [3072, 768], P('shard')
- grad_down_bias: float32 [768], P('shard')
- grad_ffn_gain: float32 [768], P('shard')
- grad_ffn_shift: float32 [768], P('shard')
Inputs may be any that keep to these rules, and one draw needn't show every extreme that they name: `seq_lengths`: each row lists the lengths of the sequences packed from the start of one group's 3072 slots; the used slots come first and each holds 1024 tokens or more, the unused ones are 0; a row sums to at most 3072; some row holds a single sequence of 3072 tokens; the slots after a row's sum are padding.
All inputs are finite; a program needn't handle non-finite values.
Results may differ from a plain program's by a relative error of at most 0.01.
Values may be sent and summed in bfloat16 or wider, within the bound.
A program may use at most 128 MiB of HBM per device.

v0:
```python
import jax
import jax.numpy as jnp
from jax import lax
from jax.sharding import PartitionSpec as P

HEADS = 12
HD = 64


epsilon = 1e-12
neg_large = -1e30


def layer_norm(value, gain, shift):
    mean_val = jnp.mean(value, axis=-1, keepdims=True)
    centred = value - mean_val
    variance = jnp.mean(centred * centred, axis=-1, keepdims=True)
    return centred * lax.rsqrt(variance + epsilon) * gain + shift


def exact_gelu(value):
    return jax.nn.gelu(value, approximate=False)


def contract_rows(left, right):
    return lax.dot_general(
        left, right, (((0,), (0,)), ((), ())), preferred_element_type=jnp.float32
    )


def contract_cols(left, right):
    return lax.dot_general(
        left, right, (((1,), (1,)), ((), ())), preferred_element_type=jnp.float32
    )


def on_device(
    inputs,
    teacher,
    seq_lengths,
    w_qkv,
    q_bias,
    v_bias,
    w_out,
    out_bias,
    attn_gain,
    attn_shift,
    w_up,
    up_bias,
    w_down,
    down_bias,
    ffn_gain,
    ffn_shift,
):
    tok_rows = inputs.shape[1]
    model_width = inputs.shape[2]
    seq_parts = lax.axis_size("seq")
    group_rows = tok_rows * seq_parts
    heads_dev = HEADS // seq_parts
    head_cols = heads_dev * HD
    block_rows = min(512, group_rows)
    nblocks = group_rows // block_rows
    score_scale = HD ** (-0.5)
    tokens = inputs[0]
    targets = teacher[0].astype(jnp.float32)
    seq_ends = jnp.cumsum(seq_lengths[0])
    all_pos = lax.iota(jnp.int32, group_rows)
    all_seg = jnp.sum((all_pos[:, None] >= seq_ends[None, :]).astype(jnp.int32), axis=1)
    own_seg = lax.dynamic_slice_in_dim(all_seg, lax.axis_index("seq") * tok_rows, tok_rows)
    live_rows = (own_seg < seq_lengths.shape[1]).astype(jnp.float32)
    live_total = lax.psum(seq_ends[-1].astype(jnp.float32), "shard")
    full_qkv, full_q_bias, full_v_bias, full_out, full_out_bias, full_attn_gain, full_attn_shift = (
        lax.all_gather(w_qkv, "shard", axis=0, tiled=True),
        lax.all_gather(q_bias, "shard", axis=0, tiled=True),
        lax.all_gather(v_bias, "shard", axis=0, tiled=True),
        lax.all_gather(w_out, "shard", axis=0, tiled=True),
        lax.all_gather(out_bias, "shard", axis=0, tiled=True),
        lax.all_gather(attn_gain, "shard", axis=0, tiled=True),
        lax.all_gather(attn_shift, "shard", axis=0, tiled=True),
    )
    bias_row = jnp.concatenate([full_q_bias, jnp.zeros_like(full_q_bias), full_v_bias]).astype(
        jnp.float32
    )
    projected = jnp.dot(tokens, full_qkv, preferred_element_type=jnp.float32) + bias_row
    projected = projected.astype(jnp.bfloat16).reshape(tok_rows, 3, seq_parts, head_cols)
    by_heads = lax.all_to_all(projected, "seq", split_axis=2, concat_axis=0, tiled=True)
    queries = by_heads[:, 0, 0]
    keys = by_heads[:, 1, 0]
    values = by_heads[:, 2, 0]

    def block_scores(q_blk, k_head, row_start):
        seg_blk = lax.dynamic_slice_in_dim(all_seg, row_start, block_rows)
        raw = contract_cols(q_blk, k_head) * score_scale
        return jnp.where(seg_blk[:, None] == all_seg[None, :], raw, neg_large)

    def attend(state_in, flat_idx):
        head_idx = flat_idx // nblocks
        row_start = flat_idx % nblocks * block_rows
        q_blk = lax.dynamic_slice(queries, (row_start, head_idx * HD), (block_rows, HD))
        k_head = lax.dynamic_slice_in_dim(keys, head_idx * HD, HD, 1)
        v_head = lax.dynamic_slice_in_dim(values, head_idx * HD, HD, 1)
        scores = block_scores(q_blk, k_head, row_start)
        row_max = jnp.max(scores, axis=1, keepdims=True)
        exp_scores = jnp.exp(scores - row_max)
        row_sum = jnp.sum(exp_scores, axis=1, keepdims=True)
        probs_low = (exp_scores / row_sum).astype(jnp.bfloat16)
        ctx_blk = jnp.dot(probs_low, v_head, preferred_element_type=jnp.float32)
        return (state_in, (ctx_blk.astype(jnp.bfloat16), (row_max + jnp.log(row_sum))[:, 0]))

    flat_ids = jnp.arange(heads_dev * nblocks, dtype=jnp.int32)
    _, (ctx_blocks, lse_blocks) = lax.scan(attend, 0, flat_ids)
    context = jnp.transpose(ctx_blocks.reshape(heads_dev, group_rows, HD), (1, 0, 2)).reshape(
        group_rows, head_cols
    )
    lse_all = lse_blocks.reshape(heads_dev, group_rows)
    merged = lax.all_to_all(
        context.reshape(group_rows, 1, head_cols), "seq", split_axis=0, concat_axis=1, tiled=True
    ).reshape(tok_rows, model_width)
    branch = jnp.dot(merged, full_out, preferred_element_type=jnp.float32) + full_out_bias.astype(
        jnp.float32
    )
    resid_one = tokens.astype(jnp.float32) + branch
    normed, norm_one_back = jax.vjp(
        layer_norm,
        resid_one,
        full_attn_gain.astype(jnp.float32),
        full_attn_shift.astype(jnp.float32),
    )
    full_up, full_up_bias, full_down, full_down_bias, full_ffn_gain, full_ffn_shift = (
        lax.all_gather(w_up, "shard", axis=0, tiled=True),
        lax.all_gather(up_bias, "shard", axis=0, tiled=True),
        lax.all_gather(w_down, "shard", axis=0, tiled=True),
        lax.all_gather(down_bias, "shard", axis=0, tiled=True),
        lax.all_gather(ffn_gain, "shard", axis=0, tiled=True),
        lax.all_gather(ffn_shift, "shard", axis=0, tiled=True),
    )
    normed_low = normed.astype(jnp.bfloat16)
    pre_act = jnp.dot(
        normed_low, full_up, preferred_element_type=jnp.float32
    ) + full_up_bias.astype(jnp.float32)
    activated, gelu_back = jax.vjp(exact_gelu, pre_act)
    act_low = activated.astype(jnp.bfloat16)
    ffn_out = jnp.dot(
        act_low, full_down, preferred_element_type=jnp.float32
    ) + full_down_bias.astype(jnp.float32)
    resid_two = normed + ffn_out
    result, norm_two_back = jax.vjp(
        layer_norm, resid_two, full_ffn_gain.astype(jnp.float32), full_ffn_shift.astype(jnp.float32)
    )
    loss_scale = float(group_rows * lax.axis_size("shard"))
    grad_result = (result - targets) * live_rows[:, None] * (loss_scale / live_total)
    back_qkv, back_out = (
        lax.all_gather(w_qkv, "shard", axis=0, tiled=True),
        lax.all_gather(w_out, "shard", axis=0, tiled=True),
    )
    back_up, back_down = (
        lax.all_gather(w_up, "shard", axis=0, tiled=True),
        lax.all_gather(w_down, "shard", axis=0, tiled=True),
    )
    grad_resid_two, grad_ffn_gain, grad_ffn_shift = norm_two_back(grad_result)
    grad_ffn_low = grad_resid_two.astype(jnp.bfloat16)
    grad_down = contract_rows(act_low, grad_ffn_low)
    grad_down_bias = jnp.sum(grad_ffn_low, axis=0, dtype=jnp.float32)
    grad_act = contract_cols(grad_ffn_low, back_down)
    (grad_pre_full,) = gelu_back(grad_act)
    grad_pre = grad_pre_full.astype(jnp.bfloat16)
    grad_up = contract_rows(normed_low, grad_pre)
    grad_up_bias = jnp.sum(grad_pre, axis=0, dtype=jnp.float32)
    grad_normed = contract_cols(grad_pre, back_up) + grad_resid_two
    grad_resid_one, grad_attn_gain, grad_attn_shift = norm_one_back(grad_normed)
    grad_branch = grad_resid_one.astype(jnp.bfloat16)
    grad_out = contract_rows(merged, grad_branch)
    grad_out_bias = jnp.sum(grad_branch, axis=0, dtype=jnp.float32)
    grad_merged = contract_cols(grad_branch, back_out).astype(jnp.bfloat16)
    grad_context = lax.all_to_all(
        grad_merged.reshape(tok_rows, seq_parts, head_cols),
        "seq",
        split_axis=1,
        concat_axis=0,
        tiled=True,
    ).reshape(group_rows, head_cols)

    def head_back(state_in, head_idx):
        k_head = lax.dynamic_slice_in_dim(keys, head_idx * HD, HD, 1)
        v_head = lax.dynamic_slice_in_dim(values, head_idx * HD, HD, 1)
        lse_head = lax.dynamic_index_in_dim(lse_all, head_idx, 0, keepdims=False)

        def block_back(sums, blk_idx):
            grad_keys, grad_values = sums
            row_start = blk_idx * block_rows
            q_blk = lax.dynamic_slice(queries, (row_start, head_idx * HD), (block_rows, HD))
            dctx_blk = lax.dynamic_slice(grad_context, (row_start, head_idx * HD), (block_rows, HD))
            lse_blk = lax.dynamic_slice_in_dim(lse_head, row_start, block_rows)
            scores = block_scores(q_blk, k_head, row_start)
            probs = jnp.exp(scores - lse_blk[:, None])
            probs_low = probs.astype(jnp.bfloat16)
            grad_probs = contract_cols(dctx_blk, v_head)
            delta = jnp.sum(grad_probs * probs, axis=1, keepdims=True)
            grad_scores = (probs * (grad_probs - delta)).astype(jnp.bfloat16)
            grad_values = grad_values + contract_rows(probs_low, dctx_blk)
            grad_keys = grad_keys + contract_rows(grad_scores, q_blk) * score_scale
            dq_blk = jnp.dot(grad_scores, k_head, preferred_element_type=jnp.float32) * score_scale
            return ((grad_keys, grad_values), dq_blk)

        zero_head = jnp.zeros((group_rows, HD), jnp.float32)
        (grad_keys, grad_values), dq_blocks = lax.scan(
            block_back, (zero_head, zero_head), jnp.arange(nblocks, dtype=jnp.int32)
        )
        return (state_in, (dq_blocks.reshape(group_rows, HD), grad_keys, grad_values))

    _, (grad_q_heads, grad_k_heads, grad_v_heads) = lax.scan(
        head_back, 0, jnp.arange(heads_dev, dtype=jnp.int32)
    )

    def side_by_side(per_head):
        return jnp.transpose(per_head, (1, 0, 2)).reshape(group_rows, head_cols)

    stacked = jnp.stack(
        [side_by_side(grad_q_heads), side_by_side(grad_k_heads), side_by_side(grad_v_heads)], axis=1
    ).astype(jnp.bfloat16)
    grad_proj = lax.all_to_all(
        stacked[:, :, None, :], "seq", split_axis=0, concat_axis=2, tiled=True
    ).reshape(tok_rows, 3 * model_width)
    grad_qkv = contract_rows(tokens, grad_proj)
    grad_q_bias = jnp.sum(grad_proj[:, :model_width], axis=0, dtype=jnp.float32)
    grad_v_bias = jnp.sum(grad_proj[:, 2 * model_width :], axis=0, dtype=jnp.float32)
    grad_inputs = grad_resid_one + contract_cols(grad_proj, back_qkv)
    owned = (
        lax.psum_scatter(grad_qkv, "shard", scatter_dimension=0, tiled=True),
        lax.psum_scatter(grad_q_bias, "shard", scatter_dimension=0, tiled=True),
        lax.psum_scatter(grad_v_bias, "shard", scatter_dimension=0, tiled=True),
        lax.psum_scatter(grad_out, "shard", scatter_dimension=0, tiled=True),
        lax.psum_scatter(grad_out_bias, "shard", scatter_dimension=0, tiled=True),
        lax.psum_scatter(grad_attn_gain, "shard", scatter_dimension=0, tiled=True),
        lax.psum_scatter(grad_attn_shift, "shard", scatter_dimension=0, tiled=True),
        lax.psum_scatter(grad_up, "shard", scatter_dimension=0, tiled=True),
        lax.psum_scatter(grad_up_bias, "shard", scatter_dimension=0, tiled=True),
        lax.psum_scatter(grad_down, "shard", scatter_dimension=0, tiled=True),
        lax.psum_scatter(grad_down_bias, "shard", scatter_dimension=0, tiled=True),
        lax.psum_scatter(grad_ffn_gain, "shard", scatter_dimension=0, tiled=True),
        lax.psum_scatter(grad_ffn_shift, "shard", scatter_dimension=0, tiled=True),
    )
    summed = (
        lax.psum(owned[0].astype(jnp.bfloat16), "seq").astype(jnp.float32),
        lax.psum(owned[1].astype(jnp.bfloat16), "seq").astype(jnp.float32),
        lax.psum(owned[2].astype(jnp.bfloat16), "seq").astype(jnp.float32),
        lax.psum(owned[3].astype(jnp.bfloat16), "seq").astype(jnp.float32),
        lax.psum(owned[4].astype(jnp.bfloat16), "seq").astype(jnp.float32),
        lax.psum(owned[5].astype(jnp.bfloat16), "seq").astype(jnp.float32),
        lax.psum(owned[6].astype(jnp.bfloat16), "seq").astype(jnp.float32),
        lax.psum(owned[7].astype(jnp.bfloat16), "seq").astype(jnp.float32),
        lax.psum(owned[8].astype(jnp.bfloat16), "seq").astype(jnp.float32),
        lax.psum(owned[9].astype(jnp.bfloat16), "seq").astype(jnp.float32),
        lax.psum(owned[10].astype(jnp.bfloat16), "seq").astype(jnp.float32),
        lax.psum(owned[11].astype(jnp.bfloat16), "seq").astype(jnp.float32),
        lax.psum(owned[12].astype(jnp.bfloat16), "seq").astype(jnp.float32),
    )
    return (
        result.astype(jnp.bfloat16)[None],
        grad_inputs.astype(jnp.bfloat16)[None],
        summed[0],
        summed[1],
        summed[2],
        summed[3],
        summed[4],
        summed[5],
        summed[6],
        summed[7],
        summed[8],
        summed[9],
        summed[10],
        summed[11],
        summed[12],
    )


def solution(mesh):
    in_specs = (
        P("shard", "seq", None),
        P("shard", "seq", None),
        P("shard", None),
        P("shard", None),
        P("shard"),
        P("shard"),
        P("shard", None),
        P("shard"),
        P("shard"),
        P("shard"),
        P("shard", None),
        P("shard"),
        P("shard", None),
        P("shard"),
        P("shard"),
        P("shard"),
    )
    out_specs = (
        P("shard", "seq", None),
        P("shard", "seq", None),
        P("shard", None),
        P("shard"),
        P("shard"),
        P("shard", None),
        P("shard"),
        P("shard"),
        P("shard"),
        P("shard", None),
        P("shard"),
        P("shard", None),
        P("shard"),
        P("shard"),
        P("shard"),
    )
    return jax.shard_map(
        on_device, mesh=mesh, in_specs=in_specs, out_specs=out_specs, check_vma=False
    )
```

profile of v0, /device:TPU:15, one launch (start us, length us, event | category | flops | bytes accessed | tf_op | source)
XLA Modules:
  0.0 1505.4 jit_solution(15992502380309811443)
XLA Ops:
  18.1 23.9 %all-reduce.18 = (bf16[768]{0:T(1024)(128)(2,1)S(1)}, bf16[768]{0:T(1024)(128)(2,1)S(1)}, bf16[768]{0:T(1024)(128)(2,1)}, bf16[768]{0:T(1024)(128)(2,1)}, bf16[7...) all-reduce(bf16[768]{0:T(1024)(128)(2,1)S(1)} %dynamic-update-slice, ...), channel_id=1, replica_groups=mesh['seq'=4,'shard'=8] {'shard'}, use_global_device_ids=true, to_apply=%add.1 | all-reduce | flops 6144 | bytes 24576
  42.0 32.6 %all-gather.6.cloned.1.call-done = bf16[768,2304]{1,0:T(8,128)(2,1)} async-done(((bf16[96,2304]{1,0:T(8,128)(2,1)}), bf16[768,2304]{1,0:T(8,128)(2,1)}) %all-gather.6.cloned.1.call-update) | async-done | bytes 3538960 | tf_op jit(solution)/shard_map/all_gather | solution.py:73
  74.6 7.1 add_convert_fusion.1
  88.3 6.0 all-to-all-start
  96.3 37.3 %all-to-all-done = bf16[768,3,4,192]{0,3,1,2:T(8,128)(2,1)S(1)} async-done(((bf16[768,3,4,192]{0,3,1,2:T(8,128)(2,1)}), bf16[768,3,4,192]{0,3,1,2:T(8,128)(2,1)S(1)}, u32[]{:S(2)}, u32[]{:S(2)}) %all-to-all-start) | async-done | bytes 3538976 | tf_op jit(solution)/shard_map/all_to_all | solution.py:86
  139.2 189.3 %while.45 = (s32[]{:T(128)}, bf16[18,512,64]{1,2,0:T(8,128)(2,1)S(1)}, f32[18,512]{1,0:T(8,128)}, s32[18]{0:T(128)S(1)}, s32[3072]{0:T(1024)S(1)}, /*index=5*/bf...) while((s32[]{:T(128)}, ...), condition=%wide.region_5.6_spmd, body=%wide.region_2.0_spmd.sunk | while | flops 416841216 | bytes 20684696 | solution.py:111
  336.3 5.9 all-to-all-start.1
  343.4 13.9 psum.98
  359.3 20.2 %all-gather = bf16[8,1,384]{2,1,0:T(2,128)(2,1)S(1)} all-gather(bf16[1,1,384]{2,1,0:T(2,128)(2,1)S(1)} %reshape.280), channel_id=1, replica_groups=mesh['seq'=4,'shard'=8] {'shard'}, dimensions={0}, use_global_device_ids=true | all-gather | bytes 6912 | tf_op jit(solution)/shard_map/all_gather | solution.py:131
  389.2 6.0 copy.186
  402.7 28.7 %multiply_convert_fusion.1 = (bf16[768,3072]{1,0:T(8,128)(2,1)}, f32[768,3072]{1,0:T(8,128)}, f32[768,3072]{1,0:T(8,128)}) fusion(f32[3072]{0:T(1024)} %bitcast.163, bf16[768,3072]{1,0:T(8,128)(2,1)} %all-gather.10.cloned.1.call-done, f32[768,768]{0,1:T(8,128)S(1)} %get-tuple-element.713, f32[768]{0:T(1024)} %convert_element_type.205, ...), kind=kOutput, calls=%fused_computation.39 | convolution fusion | flops 3782541312 | bytes 30695424 | tf_op jit(solution)/shard_map/dot_general | solution.py:138
  431.4 7.7 fusion.47
  445.8 13.5 convert_reduce_fusion
  459.4 7.6 multiply_reduce_fusion.2
  471.9 12.8 all-to-all-start.2
  488.7 10.0 all-to-all-done.2
  500.3 361.9 %while.47 = (s32[]{:T(128)}, bf16[3,3072,64]{1,2,0:T(8,128)(2,1)}, bf16[3,3072,64]{1,2,0:T(8,128)(2,1)}, bf16[3,3072,64]{1,2,0:T(8,128)(2,1)}, s32[3]{0:T(128)S(...) while((s32[]{:T(128)}, bf16[3,3072,64]{1,2,0:T(8,128)(2,1)}, ...), condition=%wide.region_19.20_spmd, body=%wide.region_15.19_spmd.sunk | while | flops 1023376896 | bytes 123100080 | solution.py:211
  509.7 109.0 %while.48 = (s32[]{:T(128)}, f32[3072,64]{0,1:T(8,128)}, f32[3072,64]{0,1:T(8,128)}, bf16[6,512,64]{1,2,0:T(8,128)(2,1)S(1)}, s32[6]{0:T(128)}, /*index=5*/s32[3...) while((s32[]{:T(128)}, f32[3072,64]{0,1:T(8,128)}, ...), condition=%wide.region_18.18_spmd.clone, body=%wide.region_16.17_spmd.clone.sunk | while | flops 1023376896 | bytes 109607288 | solution.py:206
  630.4 108.8 %while.48 = (s32[]{:T(128)}, f32[3072,64]{0,1:T(8,128)}, f32[3072,64]{0,1:T(8,128)}, bf16[6,512,64]{1,2,0:T(8,128)(2,1)S(1)}, s32[6]{0:T(128)}, /*index=5*/s32[3...) while((s32[]{:T(128)}, f32[3072,64]{0,1:T(8,128)}, ...), condition=%wide.region_18.18_spmd.clone, body=%wide.region_16.17_spmd.clone.sunk | while | flops 1023376896 | bytes 109607288 | solution.py:206
  751.0 108.8 %while.48 = (s32[]{:T(128)}, f32[3072,64]{0,1:T(8,128)}, f32[3072,64]{0,1:T(8,128)}, bf16[6,512,64]{1,2,0:T(8,128)(2,1)S(1)}, s32[6]{0:T(128)}, /*index=5*/s32[3...) while((s32[]{:T(128)}, f32[3072,64]{0,1:T(8,128)}, ...), condition=%wide.region_18.18_spmd.clone, body=%wide.region_16.17_spmd.clone.sunk | while | flops 1023376896 | bytes 109607288 | solution.py:206
  864.4 7.0 copy.198
  871.4 77.4 %all_to_all.63 = bf16[3072,3,1,192]{3,1,2,0:T(4,128)(2,1)} all-to-all(bf16[3072,3,1,192]{3,1,2,0:T(4,128)(2,1)} %copy.198), channel_id=1, replica_groups=mesh['seq'=4,'shard'=8] {'seq'}, dimensions={0} | all-to-all | bytes 7077888 | tf_op jit(solution)/shard_map/all_to_all | solution.py:221
  948.8 10.5 copy.208
  966.5 8.1 copy.209
  976.3 9.1 fusion.37
  986.6 8.7 fusion.49
  999.9 104.1 %reduce-scatter.13.cloned.1.call-done = f32[96,2304]{1,0:T(8,128)} async-done(((f32[768,2304]{1,0:T(8,128)}), f32[96,2304]{1,0:T(8,128)}) %reduce-scatter.13.cloned.1.call-update) | async-done | bytes 884752
  1106.3 164.0 %reduce-scatter.9.cloned.1.call-done = f32[96,3072]{1,0:T(8,128)} async-done(((f32[768,3072]{1,0:T(8,128)}), f32[96,3072]{1,0:T(8,128)}) %reduce-scatter.9.cloned.1.call-update) | async-done | bytes 1179664 | tf_op jit(solution)/shard_map/reduce_scatter | solution.py:236
  1272.4 164.5 %reduce-scatter.11.cloned.1.call-done = f32[384,768]{1,0:T(8,128)} async-done(((f32[3072,768]{1,0:T(8,128)}), f32[384,768]{1,0:T(8,128)}) %reduce-scatter.11.cloned.1.call-update) | async-done | bytes 1179664 | tf_op jit(solution)/shard_map/reduce_scatter | solution.py:238
  1439.1 6.7 fusion.29
  1448.5 24.5 %all-reduce.17 = (bf16[768]{0:T(1024)(128)(2,1)S(1)}, bf16[768]{0:T(1024)(128)(2,1)S(1)}, bf16[768]{0:T(1024)(128)(2,1)S(1)}, bf16[768]{0:T(1024)(128)(2,1)S(1)}...) all-reduce(f32[768]{0:T(1024)S(1)} %get-tuple-element.594, ...), channel_id=3, replica_groups=mesh['seq'=4,'shard'=8] {'shard'}, use_global_device_ids=true, to_apply=%region_23.24.clone | all-reduce | flops 9216 | bytes 55296
  1473.7 12.8 all-reduce.19
  (715 shorter events, 599.6 us)
Async XLA Ops:
  7.2 67.4 %all-gather.6.cloned.1.call-start = ((), (), s32[]{:S(2)}) async-start(), calls=%async_computation.8 | async-start | bytes 3981312 | tf_op jit(solution)/shard_map/all_gather | solution.py:73
  7.9 390.2 %all-gather.8.cloned.1.call-start = ((), (), s32[]{:S(2)}) async-start(), calls=%async_computation.9 | async-start | bytes 1327104 | tf_op jit(solution)/shard_map/all_gather | solution.py:76
  8.7 394.0 %all-gather.10.cloned.1.call-start = ((), (), s32[]{:S(2)}) async-start(), calls=%async_computation.10 | async-start | bytes 5308416 | tf_op jit(solution)/shard_map/all_gather | solution.py:130
  88.3 6.6 copy-start.47
  88.3 45.4 %all-to-all-start = ((bf16[768,3,4,192]{0,3,1,2:T(8,128)(2,1)}), bf16[768,3,4,192]{0,3,1,2:T(8,128)(2,1)S(1)}, u32[]{:S(2)}, u32[]{:S(2)}) async-start(bf16[768,3,4,192]{0,3,1,2:T(8,128)(2,1)} %copy.178), calls=%async_computation | async-start | bytes 7077888 | tf_op jit(solution)/shard_map/all_to_all | solution.py:86
  94.3 337.1 %all-gather.12.cloned.1.call-start = ((), (), s32[]{:S(2)}) async-start(), calls=%async_computation.11 | async-start | bytes 5308416 | tf_op jit(solution)/shard_map/all_gather | solution.py:132
  333.4 8.8 copy-start.45
  333.4 23.9 %copy-start.16 = (bf16[1,768,768]{2,1,0:T(8,128)(2,1)S(1)}, bf16[1,768,768]{2,1,0:T(8,128)(2,1)}, u32[]{:S(2)}) copy-start(bf16[1,768,768]{2,1,0:T(8,128)(2,1)} %param.22) | copy-start | bytes 3538948
  336.2 23.0 %copy-start.44 = (bf16[384]{0:T(512)(128)(2,1)S(1)}, bf16[384]{0:T(512)(128)(2,1)}, u32[]{:S(2)}) copy-start(bf16[384]{0:T(512)(128)(2,1)} %param.33) | copy-start | bytes 2308
  336.2 43.8 %copy-start.43 = (bf16[768]{0:T(1024)(128)(2,1)S(1)}, bf16[768]{0:T(1024)(128)(2,1)}, u32[]{:S(2)}) copy-start(bf16[768]{0:T(1024)(128)(2,1)} %get-tuple-element.669) | copy-start | bytes 4612
  336.2 43.8 %copy-start.42 = (bf16[768]{0:T(1024)(128)(2,1)S(1)}, bf16[768]{0:T(1024)(128)(2,1)}, u32[]{:S(2)}) copy-start(bf16[768]{0:T(1024)(128)(2,1)} %get-tuple-element.670) | copy-start | bytes 4612
  336.2 44.4 %copy-start.41 = (bf16[768]{0:T(1024)(128)(2,1)S(1)}, bf16[768]{0:T(1024)(128)(2,1)}, u32[]{:S(2)}) copy-start(bf16[768]{0:T(1024)(128)(2,1)} %get-tuple-element.671) | copy-start | bytes 4612
  336.2 45.0 %copy-start.15 = (bf16[1,768,768]{2,1,0:T(8,128)(2,1)S(1)}, bf16[1,768,768]{2,1,0:T(8,128)(2,1)}, u32[]{:S(2)}) copy-start(bf16[1,768,768]{2,1,0:T(8,128)(2,1)} %param.23) | copy-start | bytes 3538948
  336.3 49.4 %all-to-all-start.1 = ((bf16[4,2,73728]{2,1,0:T(2,128)(2,1)}), bf16[4,2,73728]{2,1,0:T(2,128)(2,1)}, u32[]{:S(2)}, u32[]{:S(2)}) async-start(bf16[4,2,73728]{2,1,0:T(2,128)(2,1)} %reshape.310), calls=%async_computation.1 | async-start | bytes 2359296 | tf_op jit(solution)/shard_map/all_to_all | solution.py:116
  357.2 25.9 %copy-start.40 = (bf16[768]{0:T(1024)(128)(2,1)S(1)}, bf16[768]{0:T(1024)(128)(2,1)}, u32[]{:S(2)}) copy-start(bf16[768]{0:T(1024)(128)(2,1)} %get-tuple-element.673) | copy-start | bytes 4612
  357.2 26.5 %copy-start.39 = (bf16[768]{0:T(1024)(128)(2,1)S(1)}, bf16[768]{0:T(1024)(128)(2,1)}, u32[]{:S(2)}) copy-start(bf16[768]{0:T(1024)(128)(2,1)} %get-tuple-element.674) | copy-start | bytes 4612
  400.9 66.0 %copy-start.10 = (f32[768,768]{0,1:T(8,128)}, f32[768,768]{0,1:T(8,128)S(1)}, u32[]{:S(2)}) copy-start(f32[768,768]{0,1:T(8,128)S(1)} %get-tuple-element.713) | copy-start | bytes 7077892
  401.0 66.0 %copy-start.22 = (f32[768]{0:T(1024)}, f32[768]{0:T(1024)S(1)}, u32[]{:S(2)}) copy-start(f32[768]{0:T(1024)S(1)} %broadcast_multiply_fusion.1) | copy-start | bytes 9220
  444.9 14.5 slice-start
  445.7 13.6 copy-start.13
  445.7 13.6 copy-start.29
  445.8 13.6 copy-start.33
  445.8 13.6 slice-start.1
  459.4 7.6 copy-start.25
  471.9 26.8 %all-to-all-start.2 = ((bf16[768,4,192]{0,2,1:T(8,128)(2,1)}), bf16[768,4,192]{0,2,1:T(8,128)(2,1)S(1)}, u32[]{:S(2)}, u32[]{:S(2)}) async-start(bf16[768,4,192]{0,2,1:T(8,128)(2,1)} %bitcast.160), calls=%async_computation.2 | async-start | bytes 2359296 | tf_op jit(solution)/shard_map/all_to_all | solution.py:175
  484.6 513.6 %reduce-scatter.7.cloned.1.call-start = ((), (), s32[]{:S(2)}) async-start(), calls=%async_computation.12 | async-start | bytes 2654208 | tf_op jit(solution)/shard_map/reduce_scatter | solution.py:232
  488.6 615.5 %reduce-scatter.13.cloned.1.call-start = ((), (), s32[]{:S(2)}) async-start(), calls=%async_computation.15 | async-start | bytes 7962624
  974.6 295.7 %reduce-scatter.9.cloned.1.call-start = ((), (), s32[]{:S(2)}) async-start(), calls=%async_computation.13 | async-start | bytes 10616832 | tf_op jit(solution)/shard_map/reduce_scatter | solution.py:236
  985.4 451.5 %reduce-scatter.11.cloned.1.call-start = ((), (), s32[]{:S(2)}) async-start(), calls=%async_computation.14 | async-start | bytes 10616832 | tf_op jit(solution)/shard_map/reduce_scatter | solution.py:238
  995.4 495.8 %all-reduce.23.cloned.1.call-start = ((), (), s32[]{:S(2)}) async-start(), calls=%async_computation.16 | async-start | bytes 3833856 | tf_op jit(solution)/shard_map/psum | solution.py:244
  1106.3 332.8 %copy-start.8 = (bf16[768,3,4,1,192]{0,4,2,1,3:T(8,128)(2,1)S(1)}, bf16[768,3,4,1,192]{0,4,2,1,3:T(8,128)(2,1)}, u32[]{:S(2)}) copy-start(bf16[768,3,4,1,192]{0,4,2,1,3:T(8,128)(2,1)} %copy-done.7) | copy-start | bytes 10616836
  1106.3 332.8 %copy-start.32 = (f32[768]{0:T(1024)S(1)}, f32[768]{0:T(1024)}, u32[]{:S(2)}) copy-start(f32[768]{0:T(1024)} %copy-done.31) | copy-start | bytes 9220
  (108 other events, 304.5 us)
Sparse Core Ops, SparseCore 0:
  10.2 64.3 all-gather.5
  76.7 39.7 all-gather.7
  118.7 78.0 all-gather.9
  198.8 78.3 all-gather.11
  488.7 67.4 reduce-scatter.6
  974.7 129.2 reduce-scatter.12
  1108.1 162.1 reduce-scatter.8
  1274.3 162.5 reduce-scatter.10
  1440.9 49.1 all-reduce.22
where the time goes:
time: 1530 us; the launch traced here: 1510 us
  waiting for transfers between devices  515 us (34%)
  matrix products  437 us (29%)
  local copies, waits for them, and re-layouts  199 us (13%)
  blocking collectives  173 us (11%)
  other arithmetic  82.2 us (5%)
  loops' own time  57.2 us (4%)
  starting transfers between devices  25.2 us (2%)
  between operations  18.2 us (1%)
    dot_general x58, matrix products, contract_cols(): lax.dot_general(left, right, (((1,), (1,)), ((), ())), preferred_element_...  184 us
    reduce_scatter x1, waiting for transfers between devices, on_device(): lax.psum_scatter(grad_down, 'shard', scatter_dimension=0, tiled=True)  164 us
    reduce_scatter x1, waiting for transfers between devices, on_device(): lax.psum_scatter(grad_up, 'shard', scatter_dimension=0, tiled=True)  164 us
    dot_general x40, matrix products, contract_rows(): lax.dot_general(left, right, (((0,), (0,)), ((), ())), preferred_element_...  110 us
    unnamed x10, waiting for transfers between devices  107 us
    all_to_all x1, blocking collectives, on_device(): lax.all_to_all(stacked[:, :, None, :], 'seq', split_axis=0, concat_axis=2...  77.4 us
    dot_general x18, matrix products, attend(): ctx_blk = jnp.dot(probs_low, v_head, preferred_element_type=jnp.float32)  51.2 us
    unnamed x2, blocking collectives  48.4 us
  transfers between devices with their start and end apart: 12, of which 6 were waited for; matrix products, arithmetic and copies ran while one was open for 43% of the time, Pallas kernels for 0%

commit v1 on v0

v1 whole, which is shorter than its diff:
```python
import functools
import math

import jax
import jax.numpy as jnp
from jax import lax
from jax.experimental import pallas as pl
from jax.experimental.pallas import tpu as pltpu
from jax.sharding import PartitionSpec as P

HEADS = 12
HD = 64
ROWS = 80
MESH = pl.DeviceIdType.MESH
f32 = jnp.float32
bf16 = jnp.bfloat16
epsilon = 1e-12
neg_large = -1e30
LOG2E = math.log2(math.e)
LN2 = math.log(2.0)
VMEM_LIMIT = 60 << 20

NN = (((1,), (0,)), ((), ()))
NT = (((1,), (1,)), ((), ()))
TN = (((0,), (0,)), ((), ()))


def mm(left, right, dims=NN):
    return lax.dot_general(left, right, dims, preferred_element_type=f32)


class Place:
    def __init__(self, n):
        self.n = n
        self.hi_n = 4 if n % 4 == 0 else 1
        self.lo_n = n // self.hi_n
        self.s = lax.axis_index("seq")
        self.i = lax.axis_index("shard")
        self.core = lax.rem(self.s, 2)
        self.mate = self.s + 1 - 2 * self.core
        self.far = lax.rem(self.s + 2, 4)
        self.hi = self.i // self.lo_n
        self.lo = lax.rem(self.i, self.lo_n)

    def at_hi(self, hi):
        return (self.s, hi * self.lo_n + self.lo)

    def at_lo(self, lo):
        return (self.s, self.hi * self.lo_n + lo)

    def on_seq(self, s):
        return (s, self.i)


def meet(peers):
    bar = pltpu.get_barrier_semaphore()
    for peer in peers:
        pl.semaphore_signal(bar, inc=1, device_id=peer, device_id_type=MESH)
    pl.semaphore_wait(bar, len(peers))


def rcopy(src, dst, send, recv, peer):
    return pltpu.make_async_remote_copy(
        src_ref=src, dst_ref=dst, send_sem=send, recv_sem=recv, device_id=peer, device_id_type=MESH
    )


def half(cols, core):
    return pl.ds(pl.multiple_of(core * (cols // 2), 128), cols // 2)


def gather_sems(n, hi_n, count):
    return [
        pltpu.SemaphoreType.DMA((count, hi_n)),
        pltpu.SemaphoreType.DMA((count, hi_n)),
        pltpu.SemaphoreType.DMA((count, n)),
        pltpu.SemaphoreType.DMA((count, n)),
        pltpu.SemaphoreType.DMA((count, n)),
        pltpu.SemaphoreType.DMA((count, n)),
        pltpu.SemaphoreType.DMA((count,)),
    ]


class Gather:
    def __init__(self, place, idx, src, dst, split, sems):
        self.p, self.a, self.src, self.dst, self.split = place, idx, src, dst, split
        self.s1, self.r1, self.s2, self.r2, self.s3, self.r3, self.own = sems
        self.sent = []

    def view(self, ref, core):
        return ref.at[:, half(ref.shape[-1], core)] if self.split else ref

    def start(self):
        p, a = self.p, self.a
        self.local = pltpu.make_async_copy(self.src, self.dst.at[p.i], self.own.at[a])
        self.local.start()
        mine = self.view(self.src, p.core)
        for k in range(1, p.hi_n):
            hi = lax.rem(p.hi + k, p.hi_n)
            cp = rcopy(mine, self.view(self.dst.at[p.i], p.core), self.s1.at[a, k], self.r1.at[a, p.hi], p.at_hi(hi))
            cp.start()
            self.sent.append(cp)
        self.pass_lo(0)

    def pass_lo(self, k):
        p, a = self.p, self.a
        hi = lax.rem(p.hi + k, p.hi_n)
        blk = hi * p.lo_n + p.lo
        if k:
            here = self.view(self.dst.at[blk], p.core)
            rcopy(here, here, self.s1.at[a, 0], self.r1.at[a, hi], p.at_hi(hi)).wait_recv()
        src = self.view(self.dst.at[blk] if k else self.src, p.core)
        for j in range(1, p.lo_n):
            lo = lax.rem(p.lo + j, p.lo_n)
            cp = rcopy(
                src,
                self.view(self.dst.at[blk], p.core),
                self.s2.at[a, k * p.lo_n + j],
                self.r2.at[a, blk],
                p.at_lo(lo),
            )
            cp.start()
            self.sent.append(cp)
        if k and self.split:
            self.swap(blk, k * p.lo_n)

    def swap(self, blk, slot):
        p, a = self.p, self.a
        here = self.view(self.dst.at[blk], p.core)
        cp = rcopy(here, here, self.s3.at[a, slot], self.r3.at[a, blk], p.on_seq(p.mate))
        cp.start()
        self.sent.append(cp)

    def take_lo(self, k):
        p, a = self.p, self.a
        hi = lax.rem(p.hi + k, p.hi_n)
        for j in range(1, p.lo_n):
            lo = lax.rem(p.lo + j, p.lo_n)
            blk = hi * p.lo_n + lo
            here = self.view(self.dst.at[blk], p.core)
            rcopy(here, here, self.s2.at[a, 0], self.r2.at[a, blk], p.at_lo(lo)).wait_recv()
            if self.split:
                self.swap(blk, k * p.lo_n + j)

    def finish(self):
        p, a = self.p, self.a
        if self.split:
            for k in range(p.hi_n):
                for j in range(p.lo_n):
                    if k or j:
                        blk = lax.rem(p.hi + k, p.hi_n) * p.lo_n + lax.rem(p.lo + j, p.lo_n)
                        there = self.view(self.dst.at[blk], 1 - p.core)
                        rcopy(there, there, self.s3.at[a, 0], self.r3.at[a, blk], p.on_seq(p.mate)).wait_recv()
        for cp in self.sent:
            cp.wait_send()
        self.local.wait()

    def steps(self):
        for k in range(1, self.p.hi_n):
            yield lambda k=k: self.pass_lo(k)
        for k in range(self.p.hi_n):
            yield lambda k=k: self.take_lo(k)


def peers_of(p, seq_mates):
    out = [p.at_hi(lax.rem(p.hi + k, p.hi_n)) for k in range(1, p.hi_n)]
    out += [p.at_lo(lax.rem(p.lo + j, p.lo_n)) for j in range(1, p.lo_n)]
    return out + [p.on_seq(s) for s in seq_mates]


def gather_kernel(n, splits, chunks, *refs):
    count = len(splits)
    x_ref, srcs = refs[0], refs[1 : 1 + count]
    xg_ref, dsts = refs[1 + count], refs[2 + count : 2 + 2 * count]
    sems = refs[2 + 2 * count : 9 + 2 * count]
    xsem, xs1, xr1, xs2, xr2, xown = refs[9 + 2 * count :]
    p = Place(n)
    meet(peers_of(p, (p.mate, p.far)))
    rows = x_ref.shape[0] // chunks
    part = lambda q: pl.ds(q * rows, rows)
    sent = []
    for q in range(chunks):
        cp = rcopy(x_ref.at[part(q)], xg_ref.at[p.s, part(q)], xs1.at[q], xr1.at[q], p.on_seq(p.far))
        cp.start()
        sent.append(cp)
    gathers = [Gather(p, a, srcs[a], dsts[a], splits[a], sems) for a in range(count)]
    for g in gathers:
        g.start()
    own = pltpu.make_async_copy(x_ref, xg_ref.at[p.s], xown)
    own.start()
    cp = rcopy(x_ref, xg_ref.at[p.s], xsem.at[0], xsem.at[1], p.on_seq(p.mate))
    cp.start()
    sent.append(cp)
    todo = [list(g.steps()) for g in gathers]
    first = [step for steps in todo[:2] for step in steps]
    for step in first:
        step()
    late = [step for steps in todo[2:] for step in steps]
    each = -(-len(late) // chunks) if late else 0
    for q in range(chunks):
        here = xg_ref.at[p.far, part(q)]
        rcopy(here, here, xs1.at[q], xr1.at[q], p.on_seq(p.far)).wait_recv()
        cp = rcopy(here, here, xs2.at[q], xr2.at[q], p.on_seq(p.mate))
        cp.start()
        sent.append(cp)
        for step in late[q * each : (q + 1) * each]:
            step()
    there = xg_ref.at[p.mate]
    rcopy(there, there, xsem.at[0], xsem.at[1], p.on_seq(p.mate)).wait_recv()
    for q in range(chunks):
        there = xg_ref.at[3 - p.s, part(q)]
        rcopy(there, there, xs2.at[q], xr2.at[q], p.on_seq(p.mate)).wait_recv()
    for g in gathers:
        g.finish()
    for cp in sent:
        cp.wait_send()
    own.wait()


def gather_all(x, arrays, splits, n, cid):
    hi_n = 4 if n % 4 == 0 else 1
    chunks = 4
    count = len(arrays)
    anywhere = pl.BlockSpec(memory_space=pl.ANY)
    return pl.pallas_call(
        functools.partial(gather_kernel, n, splits, chunks),
        out_shape=[jax.ShapeDtypeStruct((4,) + x.shape, x.dtype)]
        + [jax.ShapeDtypeStruct((n,) + a.shape, a.dtype) for a in arrays],
        in_specs=[anywhere] * (1 + count),
        out_specs=[anywhere] * (1 + count),
        scratch_shapes=gather_sems(n, hi_n, count)
        + [
            pltpu.SemaphoreType.DMA((2,)),
            pltpu.SemaphoreType.DMA((chunks,)),
            pltpu.SemaphoreType.DMA((chunks,)),
            pltpu.SemaphoreType.DMA((chunks,)),
            pltpu.SemaphoreType.DMA((chunks,)),
            pltpu.SemaphoreType.DMA,
        ],
        compiler_params=pltpu.CompilerParams(collective_id=cid, has_side_effects=True),
    )(x, *arrays)


def exchange_kernel(by_rows, src_ref, dst_ref, send, recv, own):
    p = Place(lax.axis_size("shard"))
    meet([p.on_seq(lax.rem(p.s + k, 4)) for k in range(1, 4)])
    if by_rows:
        rows, cols = src_ref.shape[0] // 4, src_ref.shape[1]
        take = lambda ref, k: ref.at[pl.ds(pl.multiple_of(k * rows, 16), rows)]
        put = lambda ref, k: ref.at[:, pl.ds(pl.multiple_of(k * cols, 128), cols)]
    else:
        rows, cols = src_ref.shape[0], src_ref.shape[1] // 4
        take = lambda ref, k: ref.at[:, pl.ds(pl.multiple_of(k * cols, 128), cols)]
        put = lambda ref, k: ref.at[pl.ds(pl.multiple_of(k * rows, 16), rows)]
    sent = []
    for k in (2, 1, 3):
        to = lax.rem(p.s + k, 4)
        cp = rcopy(take(src_ref, to), put(dst_ref, p.s), send.at[k], recv.at[p.s], p.on_seq(to))
        cp.start()
        sent.append(cp)
    local = pltpu.make_async_copy(take(src_ref, p.s), put(dst_ref, p.s), own)
    local.start()
    for k in (1, 2, 3):
        frm = lax.rem(p.s + k, 4)
        there = put(dst_ref, frm)
        rcopy(there, there, send.at[0], recv.at[frm], p.on_seq(frm)).wait_recv()
    for cp in sent:
        cp.wait_send()
    local.wait()


def exchange(x, by_rows, cid):
    rows, cols = x.shape
    shape = (rows // 4, cols * 4) if by_rows else (rows * 4, cols // 4)
    return pl.pallas_call(
        functools.partial(exchange_kernel, by_rows),
        out_shape=jax.ShapeDtypeStruct(shape, x.dtype),
        in_specs=[pl.BlockSpec(memory_space=pl.ANY)],
        out_specs=pl.BlockSpec(memory_space=pl.ANY),
        scratch_shapes=[
            pltpu.SemaphoreType.DMA((4,)),
            pltpu.SemaphoreType.DMA((4,)),
            pltpu.SemaphoreType.DMA,
        ],
        compiler_params=pltpu.CompilerParams(collective_id=cid, has_side_effects=True),
    )(x)


def forward_kernel(x_ref, w_ref, b_ref, augq_ref, augk_ref, augv_ref, q_ref, k_ref, v_ref, ctx_ref, lse_ref):
    toks = x_ref.shape[0]
    step = 512
    proj = mm(w_ref[0], x_ref[...], NT) + b_ref[0]
    scale = LOG2E / math.sqrt(HD)
    q_ref[0, :HD] = (proj[:HD] * scale).astype(bf16)
    q_ref[0, HD:] = augq_ref[...]
    k_ref[0, :HD] = proj[HD : 2 * HD].astype(bf16)
    k_ref[0, HD:] = augk_ref[...]
    v_ref[0, :HD] = proj[2 * HD :].astype(bf16)
    v_ref[0, HD:] = augv_ref[...]
    q = q_ref[0]
    top = jnp.full((1, toks), -3e38, f32)
    acc = jnp.zeros((ROWS, toks), f32)
    for j in range(toks // step):
        part = pl.ds(j * step, step)
        s = mm(k_ref[0, :, part], q, TN)
        new = jnp.maximum(top, jnp.max(s, axis=0, keepdims=True))
        probs = jnp.exp2(s - new).astype(bf16)
        acc = acc * jnp.exp2(top - new) + mm(v_ref[0, :, part], probs)
        top = new
    z = acc[HD : HD + 1]
    ctx_ref[...] = (acc[:HD] / z).astype(bf16)
    lse_ref[0] = jnp.broadcast_to(top + jnp.log2(z), (8, toks))


def attend(x, w_t, bias, augq, augk, augv):
    heads, _, width = w_t.shape
    toks = x.shape[0]
    whole = pl.BlockSpec((toks, width), lambda h: (0, 0))
    aug = pl.BlockSpec((ROWS - HD, toks), lambda h: (0, 0))
    head = pl.BlockSpec((1, ROWS, toks), lambda h: (h, 0, 0))
    return pl.pallas_call(
        forward_kernel,
        grid=(heads,),
        in_specs=[
            whole,
            pl.BlockSpec((1, 3 * HD, width), lambda h: (h, 0, 0)),
            pl.BlockSpec((1, 3 * HD, 1), lambda h: (h, 0, 0)),
            aug,
            aug,
            aug,
        ],
        out_specs=[
            head,
            head,
            head,
            pl.BlockSpec((HD, toks), lambda h: (h, 0)),
            pl.BlockSpec((1, 8, toks), lambda h: (h, 0, 0)),
        ],
        out_shape=[
            jax.ShapeDtypeStruct((heads, ROWS, toks), bf16),
            jax.ShapeDtypeStruct((heads, ROWS, toks), bf16),
            jax.ShapeDtypeStruct((heads, ROWS, toks), bf16),
            jax.ShapeDtypeStruct((heads * HD, toks), bf16),
            jax.ShapeDtypeStruct((heads, 8, toks), f32),
        ],
        compiler_params=pltpu.CompilerParams(vmem_limit_bytes=VMEM_LIMIT),
    )(x, w_t, bias, augq, augk, augv)


def three_parts(row):
    first = row.astype(bf16)
    rest = row - first.astype(f32)
    second = rest.astype(bf16)
    third = (rest - second.astype(f32)).astype(bf16)
    rows = lax.broadcasted_iota(jnp.int32, (8, row.shape[1]), 0)
    pick = lambda k, v: jnp.where(rows == k, jnp.broadcast_to(v.astype(f32), rows.shape), 0.0)
    return pick(0, first) + pick(1, second) + pick(2, third)


def backward_kernel(q_ref, k_ref, v_ref, ctx_ref, lse_ref, dctx_ref, out_ref, qa, da, dq):
    toks = q_ref.shape[2]
    step = 512
    qa[:HD] = q_ref[0, :HD]
    mask = q_ref[0, HD : HD + 8].astype(f32)
    zero = jnp.zeros((8, toks), f32)
    qa[HD:] = jnp.concatenate([mask, three_parts(-lse_ref[0, :1])], axis=0).astype(bf16)
    dctx = dctx_ref[...]
    delta = jnp.sum(dctx.astype(f32) * ctx_ref[...].astype(f32), axis=0, keepdims=True)
    da[:HD] = dctx
    da[HD:] = jnp.concatenate([three_parts(-delta), zero], axis=0).astype(bf16)
    q, do = qa[...], da[...]
    for j in range(toks // step):
        part = pl.ds(j * step, step)
        k = k_ref[0, :, part]
        probs = jnp.exp2(mm(k, q, TN))
        gprobs = mm(v_ref[0, :, part], do, TN)
        ds = (probs * gprobs).astype(bf16)
        probs = probs.astype(bf16)
        out_ref[0, 2 * HD :, part] = mm(do[:HD], probs, NT).astype(bf16)
        out_ref[0, HD : 2 * HD, part] = (mm(q[:HD], ds, NT) * LN2).astype(bf16)
        dq_part = mm(k[:HD], ds)
        dq[...] = dq_part if j == 0 else dq[...] + dq_part
    out_ref[0, :HD] = (dq[...] * (1.0 / math.sqrt(HD))).astype(bf16)


def attend_back(q, k, v, ctx, lse, dctx):
    heads, _, toks = q.shape
    head = pl.BlockSpec((1, ROWS, toks), lambda h: (h, 0, 0))
    rows = pl.BlockSpec((HD, toks), lambda h: (h, 0))
    return pl.pallas_call(
        backward_kernel,
        grid=(heads,),
        in_specs=[head, head, head, rows, pl.BlockSpec((1, 8, toks), lambda h: (h, 0, 0)), rows],
        out_specs=pl.BlockSpec((1, 3 * HD, toks), lambda h: (h, 0, 0)),
        out_shape=jax.ShapeDtypeStruct((heads, 3 * HD, toks), bf16),
        scratch_shapes=[
            pltpu.VMEM((ROWS, toks), bf16),
            pltpu.VMEM((ROWS, toks), bf16),
            pltpu.VMEM((HD, toks), f32),
        ],
        compiler_params=pltpu.CompilerParams(vmem_limit_bytes=VMEM_LIMIT),
    )(q, k, v, ctx, lse, dctx)


class Reduce:
    def __init__(self, p, src, out, bufs, sems, split):
        self.p, self.src, self.out, self.split = p, src, out, split
        self.acc, self.up, self.down, self.side, self.far = bufs
        (self.s0, self.r0, self.su, self.ru, self.sd, self.rd, self.sl, self.rl, self.sx) = sems
        self.sent = []

    @staticmethod
    def scratch(n, hi_n, rows, cols, split, out_seq):
        lo_n = n // hi_n
        w = cols // 2 if split else cols
        bufs = [
            pltpu.VMEM((n, rows, w), bf16),
            pltpu.VMEM((hi_n, lo_n, rows, w), bf16),
            pltpu.VMEM((hi_n, lo_n, rows, w), bf16),
            pltpu.VMEM((lo_n, rows, w), bf16),
            pltpu.VMEM((2, rows, w), bf16),
        ]
        dma = pltpu.SemaphoreType.DMA
        sems = [
            dma((hi_n,)), dma((hi_n,)), dma((hi_n,)), dma((hi_n,)), dma((hi_n,)),
            dma((hi_n,)), dma((lo_n,)), dma((lo_n,)), dma((8,)),
        ]
        return bufs, sems

    def blocks(self, ref, d):
        return ref.at[pl.ds(d * self.p.lo_n, self.p.lo_n)]

    def mine(self, ref, core):
        return ref.at[:, :, half(self.src.shape[-1], core)] if self.split else ref

    def start(self):
        p = self.p
        if self.split:
            for d in self.order():
                cp = rcopy(
                    self.mine(self.blocks(self.src, d), 1 - p.core),
                    self.blocks(self.acc, d),
                    self.s0.at[d],
                    self.r0.at[d],
                    p.on_seq(p.mate),
                )
                cp.start()
                self.sent.append(cp)

    def order(self):
        n = self.p.hi_n
        return [d for pair in zip(reversed(range(n // 2, n)), range(n // 2)) for d in pair] if n > 1 else [0]

    def chip_sum(self, d):
        p = self.p
        here = self.blocks(self.acc, d)
        own = self.mine(self.blocks(self.src, d), p.core)
        if self.split:
            rcopy(here, here, self.s0.at[d], self.r0.at[d], p.on_seq(p.mate)).wait_recv()
            here[...] = (here[...].astype(f32) + own[...].astype(f32)).astype(bf16)
        else:
            here[...] = own[...]

    def chain(self, d, buf, send, recv, step):
        p = self.p
        first = 0 if step > 0 else p.hi_n - 1
        before = (p.hi < d) if step > 0 else (p.hi > d)
        here = buf.at[d]
        acc = self.blocks(self.acc, d)

        @pl.when(before & (p.hi == first))
        def _():
            rcopy(acc, here, send.at[d], recv.at[d], p.at_hi(p.hi + step)).start()

        @pl.when(before & (p.hi != first))
        def _():
            rcopy(here, here, send.at[d], recv.at[d], p.at_hi(p.hi + step)).wait_recv()
            here[...] = (here[...].astype(f32) + acc[...].astype(f32)).astype(bf16)
            rcopy(here, here, send.at[d], recv.at[d], p.at_hi(p.hi + step)).start()

    def chain_sent(self, d, buf, send, recv, step):
        p = self.p
        before = (p.hi < d) if step > 0 else (p.hi > d)

        @pl.when(before)
        def _():
            here = buf.at[d]
            rcopy(here, here, send.at[d], recv.at[d], p.at_hi(p.hi + step)).wait_send()

    def gather_hi(self):
        p = self.p
        here = self.acc.at[pl.ds(p.hi * p.lo_n, p.lo_n)]
        total = here[...].astype(f32)
        here[...] = here[...]

        @pl.when(p.hi > 0)
        def _():
            got = self.up.at[p.hi]
            rcopy(got, got, self.su.at[0], self.ru.at[p.hi], p.at_hi(p.hi)).wait_recv()
            here[...] = (here[...].astype(f32) + got[...].astype(f32)).astype(bf16)

        @pl.when(p.hi < p.hi_n - 1)
        def _():
            got = self.down.at[p.hi]
            rcopy(got, got, self.sd.at[0], self.rd.at[p.hi], p.at_hi(p.hi)).wait_recv()
            here[...] = (here[...].astype(f32) + got[...].astype(f32)).astype(bf16)

        for j in range(1, p.lo_n):
            lo = lax.rem(p.lo + j, p.lo_n)
            cp = rcopy(
                self.acc.at[p.hi * p.lo_n + lo], self.side.at[p.lo], self.sl.at[j], self.rl.at[p.lo], p.at_lo(lo)
            )
            cp.start()
            self.sent.append(cp)

    def gather_lo(self):
        p = self.p
        total = self.acc[p.i].astype(f32)
        for j in range(1, p.lo_n):
            lo = lax.rem(p.lo + j, p.lo_n)
            got = self.side.at[lo]
            rcopy(got, got, self.sl.at[0], self.rl.at[lo], p.at_lo(lo)).wait_recv()
            total = total + got[...].astype(f32)
        self.far[0] = total.astype(bf16)
        if self.split:
            cp = rcopy(self.far.at[0], self.far.at[1], self.sx.at[0], self.sx.at[1], p.on_seq(p.far))
            cp.start()
            self.sent.append(cp)
        else:
            for k in range(1, 4):
                to = lax.rem(p.s + k, 4)
                cp = rcopy(self.far.at[0], self.out.at[p.s], self.sx.at[k], self.sx.at[4 + p.s], p.on_seq(to))
                cp.start()
                self.sent.append(cp)
            self.out[p.s] = self.far[0]

    def gather_chips(self):
        p = self.p
        if self.split:
            got = self.far.at[1]
            rcopy(got, got, self.sx.at[0], self.sx.at[1], p.on_seq(p.far)).wait_recv()
            where = half(self.src.shape[-1], p.core)
            self.out[:, where] = (self.far[0].astype(f32) + self.far[1].astype(f32)).astype(bf16)
            cp = rcopy(self.out.at[:, where], self.out.at[:, where], self.sx.at[2], self.sx.at[3], p.on_seq(p.mate))
            cp.start()
            self.sent.append(cp)

    def finish(self):
        p = self.p
        if self.split:
            there = self.out.at[:, half(self.src.shape[-1], 1 - p.core)]
            rcopy(there, there, self.sx.at[2], self.sx.at[3], p.on_seq(p.mate)).wait_recv()
        else:
            for k in range(1, 4):
                frm = lax.rem(p.s + k, 4)
                there = self.out.at[frm]
                rcopy(there, there, self.sx.at[0], self.sx.at[4 + frm], p.on_seq(frm)).wait_recv()
        for cp in self.sent:
            cp.wait_send()
        for d in range(1, p.hi_n):
            self.chain_sent(d, self.up, self.su, self.ru, 1)
            self.chain_sent(d - 1, self.down, self.sd, self.rd, -1)

    def steps(self):
        n = self.p.hi_n
        for d in self.order():
            yield lambda d=d: self.chip_sum(d)
        for k in range(1, n):
            yield lambda k=k: self.chain(n - k, self.up, self.su, self.ru, 1)
            yield lambda k=k: self.chain(k - 1, self.down, self.sd, self.rd, -1)
        yield self.gather_hi
        yield self.gather_lo
        yield self.gather_chips


def reduce_peers(p):
    out = [p.at_hi(lax.rem(p.hi + k, p.hi_n)) for k in range(1, p.hi_n)]
    out += [p.at_lo(lax.rem(p.lo + j, p.lo_n)) for j in range(1, p.lo_n)]
    return out + [p.on_seq(lax.rem(p.s + k, 4)) for k in range(1, 4)]


def reduce_kernel(n, splits, *refs):
    count = len(splits)
    srcs, outs = refs[:count], refs[count : 2 * count]
    rest = refs[2 * count :]
    p = Place(n)
    meet(reduce_peers(p))
    reds = [Reduce(p, srcs[a], outs[a], rest[14 * a : 14 * a + 5], rest[14 * a + 5 : 14 * a + 14], splits[a]) for a in range(count)]
    for r in reds:
        r.start()
    for row in zip(*[list(r.steps()) for r in reds]):
        for step in row:
            step()
    for r in reds:
        r.finish()


def reduce_all(arrays, splits, n, cid):
    hi_n = 4 if n % 4 == 0 else 1
    vm = pl.BlockSpec(memory_space=pltpu.VMEM)
    scratch, outs = [], []
    for a, split in zip(arrays, splits):
        bufs, sems = Reduce.scratch(n, hi_n, a.shape[1], a.shape[2], split, not split)
        scratch += bufs + sems
        outs.append(jax.ShapeDtypeStruct(a.shape[1:] if split else (4,) + a.shape[1:], bf16))
    return pl.pallas_call(
        functools.partial(reduce_kernel, n, splits),
        out_shape=outs,
        in_specs=[vm] * len(arrays),
        out_specs=[vm] * len(arrays),
        scratch_shapes=scratch,
        compiler_params=pltpu.CompilerParams(collective_id=cid, has_side_effects=True, vmem_limit_bytes=VMEM_LIMIT),
    )(*arrays)


def finish_kernel(n, part_ref, resid_ref, vec_ref, out_ref, vout_ref, near, far, give, vin, vseq, sems, vs, vr, ws, wr):
    p = Place(n)
    seq_mates = [p.on_seq(lax.rem(p.s + k, 4)) for k in range(1, 4)]
    others = [(p.s, lax.rem(p.i + k, n)) for k in range(1, n)]
    meet(seq_mates + others)
    rows = part_ref.shape[0] // 4
    block = lambda s: part_ref.at[pl.ds(pl.multiple_of(s * rows, 16), rows)]
    sent = []
    beyond = lax.rem(p.mate + 2, 4)
    for slot, to in ((0, beyond), (1, p.mate)):
        cp = rcopy(block(to), near.at[slot], sems.at[slot], sems.at[2 + slot], p.on_seq(p.mate))
        cp.start()
        sent.append(cp)
    for k in range(1, n):
        to = lax.rem(p.i + k, n)
        cp = rcopy(vec_ref.at[to], vin.at[p.i], vs.at[k], vr.at[p.i], (p.s, to))
        cp.start()
        sent.append(cp)
    vin[p.i] = vec_ref[p.i]
    rcopy(near.at[0], near.at[0], sems.at[0], sems.at[2], p.on_seq(p.mate)).wait_recv()
    give[...] = (near[0].astype(f32) + block(p.far)[...].astype(f32)).astype(bf16)
    cp = rcopy(give, far, sems.at[4], sems.at[5], p.on_seq(p.far))
    cp.start()
    sent.append(cp)
    rcopy(near.at[1], near.at[1], sems.at[1], sems.at[3], p.on_seq(p.mate)).wait_recv()
    total = resid_ref[...] + near[1].astype(f32) + block(p.s)[...].astype(f32)
    for k in range(1, n):
        frm = lax.rem(p.i + k, n)
        there = vin.at[frm]
        rcopy(there, there, vs.at[0], vr.at[frm], (p.s, frm)).wait_recv()
    vseq[p.s] = jnp.sum(vin[...], axis=0)
    for k in range(1, 4):
        to = lax.rem(p.s + k, 4)
        cp = rcopy(vseq.at[p.s], vseq.at[p.s], ws.at[k], wr.at[p.s], p.on_seq(to))
        cp.start()
        sent.append(cp)
    rcopy(far, far, sems.at[4], sems.at[5], p.on_seq(p.far)).wait_recv()
    out_ref[...] = (total + far[...].astype(f32)).astype(bf16)
    for k in range(1, 4):
        frm = lax.rem(p.s + k, 4)
        there = vseq.at[frm]
        rcopy(there, there, ws.at[0], wr.at[frm], p.on_seq(frm)).wait_recv()
    vout_ref[...] = (vseq[0] + vseq[1]) + (vseq[2] + vseq[3])
    for cp in sent:
        cp.wait_send()


def finish(part, resid, vec, n, cid):
    rows, width = resid.shape
    vm = pl.BlockSpec(memory_space=pltpu.VMEM)
    dma = pltpu.SemaphoreType.DMA
    return pl.pallas_call(
        functools.partial(finish_kernel, n),
        out_shape=[jax.ShapeDtypeStruct((rows, width), bf16), jax.ShapeDtypeStruct(vec.shape[1:], f32)],
        in_specs=[vm] * 3,
        out_specs=[vm] * 2,
        scratch_shapes=[
            pltpu.VMEM((2, rows, width), bf16),
            pltpu.VMEM((rows, width), bf16),
            pltpu.VMEM((rows, width), bf16),
            pltpu.VMEM(vec.shape, f32),
            pltpu.VMEM((4,) + vec.shape[1:], f32),
            dma((6,)),
            dma((n,)),
            dma((n,)),
            dma((4,)),
            dma((4,)),
        ],
        compiler_params=pltpu.CompilerParams(collective_id=cid, has_side_effects=True, vmem_limit_bytes=VMEM_LIMIT),
    )(part, resid, vec)


def layer_norm(value, gain, shift):
    mean_val = jnp.mean(value, axis=-1, keepdims=True)
    centred = value - mean_val
    variance = jnp.mean(centred * centred, axis=-1, keepdims=True)
    return centred * lax.rsqrt(variance + epsilon) * gain + shift


def exact_gelu(value):
    return jax.nn.gelu(value, approximate=False)


def on_device(
    inputs, teacher, seq_lengths, w_qkv, q_bias, v_bias, w_out, out_bias, attn_gain, attn_shift, w_up, up_bias,
    w_down, down_bias, ffn_gain, ffn_shift,
):
    n = lax.axis_size("shard")
    s = lax.axis_index("seq")
    toks, width = inputs.shape[1:]
    group = 4 * toks
    hidden = w_up.shape[1]
    rows = w_qkv.shape[0]
    heads = HEADS // 4
    tokens = inputs[0]
    lens = seq_lengths[0]
    ends = [lens[0], lens[0] + lens[1], lens[0] + lens[1] + lens[2]]

    own_w = lax.dynamic_index_in_dim(w_qkv.reshape(rows, 3, 4, heads, HD), s, 2, keepdims=False)
    own_w = jnp.transpose(own_w, (0, 2, 1, 3)).reshape(rows, heads * 3 * HD)
    live = jnp.stack([ends[2] // 64, lax.rem(ends[2], 64)]).astype(bf16)
    small = jnp.concatenate(
        [q_bias[None], v_bias[None], out_bias[None], attn_gain[None], attn_shift[None], down_bias[None], ffn_gain[None],
         ffn_shift[None], up_bias.reshape(hidden // width, rows), jnp.broadcast_to(live[:, None], (2, rows))], axis=0
    )
    small = jnp.pad(small, ((0, 16 - small.shape[0]), (0, -rows % 128)))
    xg, wq_g, small_g, wo_g, up_g, down_g = gather_all(
        tokens, (own_w, small, w_out, w_up, w_down), (False, False, True, True, True), n, 1
    )
    x_all = xg.reshape(group, width)
    wq = wq_g.reshape(width, heads * 3 * HD)
    full_out = wo_g.reshape(width, width)
    full_up = up_g.reshape(width, hidden)
    full_down = down_g.reshape(hidden, width)
    vecs = jnp.transpose(small_g[:, :, :rows], (1, 0, 2)).astype(f32)
    rest = vecs[:8].reshape(8, width)
    b_q, b_v, b_out, g_attn, s_attn, b_down, g_ffn, s_ffn = [rest[k] for k in range(8)]
    b_up = jnp.transpose(vecs[8 : 8 + hidden // width], (1, 0, 2)).reshape(hidden)
    live_total = jnp.sum(vecs[8 + hidden // width, :, 0]) * 64.0 + jnp.sum(vecs[9 + hidden // width, :, 0])

    own_q = lax.dynamic_slice_in_dim(b_q, s * heads * HD, heads * HD).reshape(heads, 1, HD)
    own_v = lax.dynamic_slice_in_dim(b_v, s * heads * HD, heads * HD).reshape(heads, 1, HD)
    bias = jnp.concatenate([own_q, jnp.zeros_like(own_q), own_v], axis=1).reshape(heads, 3 * HD, 1)

    pos = lax.broadcasted_iota(jnp.int32, (16, group), 1)
    row = lax.broadcasted_iota(jnp.int32, (16, group), 0)
    seg = sum((pos >= e).astype(jnp.int32) for e in ends)
    augq = jnp.where((row < 4) & (seg != row), neg_large, 0.0).astype(bf16)
    augk = jnp.where((row < 4) & (seg == row) | (row >= 8) & (row < 11), 1.0, 0.0).astype(bf16)
    augv = jnp.where(row < 3, 1.0, 0.0).astype(bf16)

    w_t = jnp.transpose(wq).reshape(heads, 3 * HD, width)
    q, k, v, ctx, lse = attend(x_all, w_t, bias, augq, augk, augv)
    merged = exchange(ctx, False, 2)

    branch = mm(merged, full_out, TN) + b_out
    resid_one = tokens.astype(f32) + branch
    normed, norm_one_back = jax.vjp(layer_norm, resid_one, g_attn, s_attn)
    normed_low = normed.astype(bf16)
    pre_act = mm(normed_low, full_up) + b_up
    activated, gelu_back = jax.vjp(exact_gelu, pre_act)
    act_low = activated.astype(bf16)
    resid_two = normed + mm(act_low, full_down) + b_down
    result, norm_two_back = jax.vjp(layer_norm, resid_two, g_ffn, s_ffn)
    own_pos = s * toks + lax.iota(jnp.int32, toks)
    live_rows = (own_pos < ends[2]).astype(f32)
    loss_scale = float(group * n)
    grad_result = (result - teacher[0].astype(f32)) * live_rows[:, None] * (loss_scale / live_total)
    grad_resid_two, d_ffn_gain, d_ffn_shift = norm_two_back(grad_result)
    grad_ffn_low = grad_resid_two.astype(bf16)
    d_down = mm(act_low, grad_ffn_low, TN).astype(bf16)
    d_down_bias = jnp.sum(grad_ffn_low, axis=0, dtype=f32)
    (grad_pre_full,) = gelu_back(mm(grad_ffn_low, full_down, NT))
    grad_pre = grad_pre_full.astype(bf16)
    d_up = mm(normed_low, grad_pre, TN).astype(bf16)
    d_up_bias = jnp.sum(grad_pre, axis=0, dtype=f32)
    grad_normed = mm(grad_pre, full_up, NT) + grad_resid_two
    grad_resid_one, d_attn_gain, d_attn_shift = norm_one_back(grad_normed)
    grad_branch = grad_resid_one.astype(bf16)
    d_out = mm(merged, grad_branch).astype(bf16)
    d_out_bias = jnp.sum(grad_branch, axis=0, dtype=f32)
    grad_merged = mm(full_out, grad_branch, NT).astype(bf16)
    dctx = exchange(grad_merged, True, 3)

    d_up_r, d_down_r, d_out_r = reduce_all(
        (d_up.reshape(n, rows, hidden), d_down.reshape(n, hidden // n, width), d_out.reshape(n, rows, width)),
        (True, True, True), n, 4,
    )
    dqkv = attend_back(q, k, v, ctx, lse, dctx).reshape(heads * 3 * HD, group)
    d_qkv = lax.dot_general(x_all, dqkv, (((0,), (1,)), ((), ())), preferred_element_type=f32).astype(bf16)
    part = lax.dot_general(dqkv, wq, (((0,), (1,)), ((), ())), preferred_element_type=f32).astype(bf16)
    d_bias = jnp.sum(dqkv, axis=1, dtype=f32).reshape(heads, 3, HD)
    place = lambda v: lax.dynamic_update_slice_in_dim(jnp.zeros((width,), f32), v.reshape(-1), s * heads * HD, 0)
    flat = jnp.stack(
        [place(d_bias[:, 0]), place(d_bias[:, 2]), d_out_bias, d_attn_gain, d_attn_shift, d_down_bias, d_ffn_gain, d_ffn_shift]
    )
    vec = jnp.concatenate(
        [jnp.transpose(flat.reshape(8, n, rows), (1, 0, 2)), d_up_bias.reshape(n, hidden // width, rows)], axis=1
    )
    vec = jnp.pad(vec, ((0, 0), (0, 16 - vec.shape[1]), (0, -rows % 128)))
    (d_qkv_r,) = reduce_all((d_qkv.reshape(n, rows, heads * 3 * HD),), (False,), n, 5)
    grad_in, vsum = finish(part, grad_resid_one, vec, n, 6)

    d_qkv_out = jnp.transpose(d_qkv_r.reshape(4, rows, heads, 3, HD), (1, 3, 0, 2, 4)).reshape(rows, 3 * width)
    vsum = vsum[:, :rows]
    d_up_bias = vsum[8 : 8 + hidden // width].reshape(hidden // n)
    return (
        result.astype(bf16)[None], grad_in[None], d_qkv_out.astype(f32), vsum[0], vsum[1], d_out_r.astype(f32), vsum[2],
        vsum[3], vsum[4], d_up_r.astype(f32), d_up_bias, d_down_r.astype(f32), vsum[5], vsum[6], vsum[7],
    )


def solution(mesh):
    tokens, matrix, vector = P("shard", "seq", None), P("shard", None), P("shard")
    in_specs = (tokens, tokens, matrix, matrix, vector, vector, matrix, vector, vector, vector, matrix, vector, matrix,
                vector, vector, vector)
    out_specs = (tokens, tokens, matrix, vector, vector, matrix, vector, vector, vector, matrix, vector, matrix, vector,
                 vector, vector)
    return jax.shard_map(on_device, mesh=mesh, in_specs=in_specs, out_specs=out_specs, check_vma=False)
```

time: 1530 us -> 644 us (0.42)
  waiting for transfers between devices: 515 us -> 0 us
  Pallas kernels: 0 us -> 462 us
  matrix products: 437 us -> 94 us
  blocking collectives: 173 us -> 0 us
  local copies, waits for them, and re-layouts: 199 us -> 48.6 us
  other arithmetic: 82.2 us -> 23.9 us
  loops' own time: 57.2 us -> 0 us
  starting transfers between devices: 25.2 us -> 0 us
    pallas_call x0 -> x8, Pallas kernels: none -> 462 us  [the longest x2 175 us: reduce_all(): pl.pallas_call(functools.partial(reduce_kernel, n, splits), out_shape=out...]
    dot_general x138 -> x11, matrix products: 437 us -> 94 us  [the longest x9 79.3 us: mm(): return lax.dot_general(left, right, dims, preferred_element_type=f32)]
    reduce_scatter x3 -> x0, waiting for transfers between devices: 328 us -> none  [the longest x1 164 us: on_device(): lax.psum_scatter(grad_down, 'shard', scatter_dimension=0, tiled=True)]
    unnamed x10 -> x0, waiting for transfers between devices: 107 us -> none
    all_to_all x1 -> x0, blocking collectives: 77.4 us -> none  [on_device(): lax.all_to_all(stacked[:, :, None, :], 'seq', split_axis=0, concat_axis=2...]
    dynamic_slice x102 -> x2, local copies, waits for them, and re-layouts: 67.8 us -> 0.15 us  [the longest x1 0.08 us: on_device(): lax.dynamic_slice_in_dim(b_v, s * heads * HD, heads * HD)]
    another operation x5 -> x0, loops' own time: 57.2 us -> none  [the longest x1 35.8 us: on_device(): _, (ctx_blocks, lse_blocks) = lax.scan(attend, 0, flat_ids)]
    unnamed x2 -> x0, blocking collectives: 48.4 us -> none
  transfers between devices with their start and end apart: 12 -> 0, of which waited for: 6 -> 0; matrix products, arithmetic and copies ran while one was open for 43% -> 0% of each run, Pallas kernels for 0% -> 0%
where the time goes in v1:
time: 644 us; the launch traced here: 633 us
  Pallas kernels  462 us (72%)
  matrix products  94 us (15%)
  local copies, waits for them, and re-layouts  48.6 us (8%)
  other arithmetic  23.9 us (4%)
    pallas_call x2, Pallas kernels, reduce_all(): pl.pallas_call(functools.partial(reduce_kernel, n, splits), out_shape=out...  175 us
    pallas_call x1, Pallas kernels, gather_all(): pl.pallas_call(functools.partial(gather_kernel, n, splits, chunks), out_s...  104 us
    dot_general x9, matrix products, mm(): return lax.dot_general(left, right, dims, preferred_element_type=f32)  79.3 us
    pallas_call x1, Pallas kernels, attend_back(): pl.pallas_call(backward_kernel, grid=(heads,), in_specs=[head, head, head...  76.3 us
    pallas_call x1, Pallas kernels, attend(): pl.pallas_call(forward_kernel, grid=(heads,), in_specs=[whole, pl.BlockSp...  40.5 us
    pallas_call x1, Pallas kernels, finish(): pl.pallas_call(functools.partial(finish_kernel, n), out_shape=[jax.ShapeD...  35.6 us
    pallas_call x2, Pallas kernels, exchange(): pl.pallas_call(functools.partial(exchange_kernel, by_rows), out_shape=jax...  31.1 us
    another operation x13, local copies, waits for them, and re-layouts, on_device(): jnp.stack([place(d_bias[:, 0]), place(d_bias[:, 2]), d_out_bias, d_attn_g...  16 us

profile of v1, /device:TPU:15, one launch (start us, length us, event | category | flops | bytes accessed | tf_op | source)
XLA Modules:
  0.0 633.5 jit_solution(6341151921730707495)
XLA Ops:
  8.5 103.7 %shard_map.271 = (bf16[4,768,768]{2,1,0:T(8,128)(2,1)}, bf16[8,96,576]{2,1,0:T(8,128)(2,1)}, bf16[8,16,128]{2,1,0:T(8,128)(2,1)}, bf16[8,96,768]{2,1,0:T(8,128)(...) custom-call(bf16[768,768]{1,0:T(8,128)(2,1)} %bitcast.98, bf16[96,576]{1,0:T(8,128)(2,1)} %copy.47.refs_1_, ...), custom_call_target="tpu_custom_call" | custom-call | tf_op jit(solution)/shard_map/pallas_call | solution.py:225
  114.5 2.2 copy.48
  120.4 40.5 %shard_map.272 = (bf16[3,80,3072]{2,1,0:T(8,128)(2,1)}, bf16[3,80,3072]{2,1,0:T(8,128)(2,1)}, bf16[3,80,3072]{2,1,0:T(8,128)(2,1)}, bf16[192,3072]{1,0:T(8,128)(2,1)}, f32[3,8,3072]{2,1,0:T(8,128)}) custom-call(bf16[3072,768]{1,0:T(8,128)(2,1)} %bitcast.90, bf16[3,192,768]{2,1,0:T(8,128)(2,1)} %bitcast.97, f32[3,192,1]{2,1,0:T(8,128)} %reshape.253.b_ref, ...), custom_call_target="tpu_custom_call" | custom-call | tf_op jit(solution)/shard_map/pallas_call | solution.py:321
  161.0 15.6 %shard_map.273 = bf16[768,768]{1,0:T(8,128)(2,1)} custom-call(bf16[192,3072]{1,0:T(8,128)(2,1)} %get-tuple-element.34.src_ref.ctx_ref), custom_call_target="tpu_custom_call" | custom-call | tf_op jit(solution)/shard_map/pallas_call | solution.py:275
  176.6 3.5 fusion.28
  181.4 27.5 %multiply_convert_fusion = (bf16[768,3072]{1,0:T(8,128)(2,1)S(1)}, f32[768,3072]{1,0:T(8,128)}, f32[768,3072]{1,0:T(8,128)}) fusion(f32[3072]{0:T(1024)S(1)} %copy-done.23, bf16[768,3072]{1,0:T(8,128)(2,1)} %bitcast.114, f32[768,768]{1,0:T(8,128)S(1)} %get-tuple-element.122, f32[768]{0:T(1024)S(1)} %add.133, f32[768]{0:T(1024)S(1)} %mul.174, ...), kind=kOutput, calls=%fused_computation.4 | convolution fusion | flops 3782541312 | bytes 30695424 | tf_op jit(solution)/shard_map/dot_general | solution.py:29
  209.0 9.5 %fusion.29 = (f32[768]{0:T(1024)}, f32[768,768]{1,0:T(8,128)S(1)}) fusion(f32[768]{0:T(1024)S(1)} %add.140, bf16[768,3072]{1,0:T(8,128)(2,1)S(1)} %get-tuple-element.105, bf16[3072,768]{1,0:T(8,128)(2,1)} %bitcast.118, f32[768]{0:T(1024)S(1)} %add.133, f32[768]{0:T(1024)S(1)} %mul.174, f32[768]{0:T(1024)S(1)} %fusion.16, f32[768,768]{1,0:T(8,128)} %copy-done.1, ...), kind=kOutput, calls=%fused_computation.111 | convolution fusion | flops 3628006656 | bytes 14174208 | tf_op jit(solution)/shard_map/dot_general | solution.py:29
  218.4 1.5 slice_reduce_fusion
  224.5 2.6 fusion.10
  227.1 2.4 fusion.25
  230.4 12.8 %convert_reduce_fusion = (f32[3072]{0:T(1024)}, bf16[768,3072]{1,0:T(8,128)(2,1)S(1)}) fusion(f32[768,3072]{1,0:T(8,128)} %get-tuple-element.106, f32[768,3072]{1,0:T(8,128)} %get-tuple-element.123, f32[3072]{0:T(1024)S(1)} %copy-done.24, bf16[768,768]{1,0:T(8,128)(2,1)S(1)} %get-tuple-element.96, bf16[3072,768]{1,0:T(8,128)(2,1)} %bitcast.119), kind=kOutput, calls=%fused_computation.2 | convolution fusion | flops 3663983616 | bytes 29515776 | tf_op jit(solution)/shard_map/dot_general | solution.py:29
  243.2 5.1 multiply_reduce_fusion.1
  250.1 1.4 copy-done.4
  251.5 2.2 convolution_convert_fusion.4.src_ref
  253.7 15.6 %shard_map.274.dctx_ref = bf16[192,3072]{1,0:T(8,128)(2,1)} custom-call(bf16[768,768]{1,0:T(8,128)(2,1)} %convolution_convert_fusion.4.src_ref), custom_call_target="tpu_custom_call" | custom-call | tf_op jit(solution)/shard_map/pallas_call | solution.py:275
  269.3 76.3 %shard_map.275 = bf16[3,192,3072]{2,1,0:T(8,128)(2,1)} custom-call(bf16[3,80,3072]{2,1,0:T(8,128)(2,1)} %get-tuple-element.38.q_ref, bf16[3,80,3072]{2,1,0:T(8,128)(2,1)} %get-tuple-element.39.k_ref, bf16[3,80,3072]{2,1,0:T(8,128)(2,1)} %get-tuple-element.40.v_ref, bf16[192,3072]{1,0:T(8,128)(2,1)} %get-tuple-element.34.src_ref.ctx_ref, ...), custom_call_target="tpu_custom_call" | custom-call | tf_op jit(solution)/shard_map/pallas_call | solution.py:390
  345.6 8.5 %convolution_convert_fusion.2.part_ref = bf16[3072,768]{1,0:T(8,128)(2,1)} fusion(bf16[576,3072]{1,0:T(8,128)(2,1)} %bitcast.88, bf16[768,576]{1,0:T(8,128)(2,1)} %bitcast.102), kind=kOutput, calls=%fused_computation.21 | convolution fusion | flops 2720268288 | bytes 9142272 | tf_op jit(solution)/shard_map/dot_general | solution.py:786
  357.4 1.4 slice_reduce_fusion.10
  378.7 1.4 stack.56
  380.1 1.4 select_maximum_fusion.vec_ref
  381.5 35.6 %shard_map.276 = (bf16[768,768]{1,0:T(8,128)(2,1)}, f32[16,128]{1,0:T(8,128)}) custom-call(bf16[3072,768]{1,0:T(8,128)(2,1)} %convolution_convert_fusion.2.part_ref, f32[768,768]{1,0:T(8,128)} %copy-done.4, f32[8,16,128]{2,1,0:T(8,128)} %select_maximum_fusion.vec_ref), custom_call_target="tpu_custom_call" | custom-call | tf_op jit(solution)/shard_map/pallas_call | solution.py:667
  417.1 6.1 convolution_convert_fusion.5
  423.2 2.2 copy.51
  425.5 37.4 %shard_map.277 = bf16[4,96,576]{2,1,0:T(8,128)(2,1)} custom-call(bf16[8,96,576]{2,1,0:T(8,128)(2,1)} %bitcast.96), custom_call_target="tpu_custom_call" | custom-call | tf_op jit(solution)/shard_map/pallas_call | solution.py:606
  465.3 2.6 copy.54
  467.9 1.5 slice_bitcast_fusion.1
  469.4 8.5 %convolution_convert_fusion.1 = bf16[768,3072]{1,0:T(8,128)(2,1)} fusion(bf16[768,3072]{1,0:T(8,128)(2,1)} %copy-done.28, f32[768,768]{1,0:T(8,128)S(1)} %copy-done.3, f32[768]{0:T(1024)S(1)} %copy-done.26, f32[768]{0:T(1024)S(1)} %copy-done.19, f32[768]{0:T(1024)S(1)} %copy-done.22, f32[768]{0:T(1024)S(1)} %copy-done.15), kind=kOutput, calls=%fused_computation.20 | convolution fusion | flops 3629187072 | bytes 11808768 | tf_op jit(solution)/shard_map/dot_general | solution.py:29
  478.0 8.2 %convolution_convert_fusion = bf16[3072,768]{1,0:T(8,128)(2,1)} fusion(bf16[768,3072]{1,0:T(8,128)(2,1)} %copy-done.29, bf16[768,768]{1,0:T(8,128)(2,1)S(1)} %copy-done.9), kind=kOutput, calls=%fused_computation.19 | convolution fusion | flops 3626237952 | bytes 10616832 | tf_op jit(solution)/shard_map/dot_general | solution.py:29
  486.1 2.1 convolution_convert_fusion.3
  488.3 137.6 %shard_map.278 = (bf16[96,3072]{1,0:T(8,128)(2,1)}, bf16[384,768]{1,0:T(8,128)(2,1)}, bf16[96,768]{1,0:T(8,128)(2,1)}) custom-call(bf16[8,96,3072]{2,1,0:T(8,128)(2,1)} %bitcast.94, bf16[8,384,768]{2,1,0:T(8,128)(2,1)} %bitcast.95, bf16[8,96,768]{2,1,0:T(8,128)(2,1)} %bitcast.100), custom_call_target="tpu_custom_call" | custom-call | tf_op jit(solution)/shard_map/pallas_call | solution.py:606
  625.9 1.8 convert_element_type.154
  627.7 2.2 convert_element_type.155
  (137 shorter events, 48.1 us)
Async XLA Ops:
  113.0 48.0 %copy-start.13 = (f32[16,8,96]{2,0,1:T(8,128)}, f32[16,8,96]{2,0,1:T(8,128)S(1)}, u32[]{:S(2)}) copy-start(f32[16,8,96]{2,0,1:T(8,128)S(1)} %convert_bitcast_fusion) | copy-start | bytes 147460
  161.0 15.6 %copy-start.7 = (bf16[1,768,768]{2,1,0:T(8,128)(2,1)S(1)}, bf16[1,768,768]{2,1,0:T(8,128)(2,1)}, u32[]{:S(2)}) copy-start(bf16[1,768,768]{2,1,0:T(8,128)(2,1)} %param.16) | copy-start | bytes 3538948
  180.1 28.9 %copy-start.1 = (f32[768,768]{1,0:T(8,128)}, f32[768,768]{1,0:T(8,128)S(1)}, u32[]{:S(2)}) copy-start(f32[768,768]{1,0:T(8,128)S(1)} %get-tuple-element.122) | copy-start | bytes 7077892
  180.1 1.3 copy-start.23
  180.2 28.8 %copy-start.25 = (f32[768]{0:T(1024)}, f32[768]{0:T(1024)S(1)}, u32[]{:S(2)}) copy-start(f32[768]{0:T(1024)S(1)} %add.133) | copy-start | bytes 9220
  180.2 28.7 %copy-start.17 = (f32[768]{0:T(1024)}, f32[768]{0:T(1024)S(1)}, u32[]{:S(2)}) copy-start(f32[768]{0:T(1024)S(1)} %mul.174) | copy-start | bytes 9220
  181.0 67.4 %copy-start.14 = (f32[768]{0:T(1024)}, f32[768]{0:T(1024)S(1)}, u32[]{:S(2)}) copy-start(f32[768]{0:T(1024)S(1)} %broadcast_multiply_fusion.1) | copy-start | bytes 9220
  181.4 27.6 %copy-start.20 = (f32[768]{0:T(1024)}, f32[768]{0:T(1024)S(1)}, u32[]{:S(2)}) copy-start(f32[768]{0:T(1024)S(1)} %fusion.16) | copy-start | bytes 9220
  208.9 9.5 %copy-start.29 = (bf16[768,3072]{1,0:T(8,128)(2,1)}, bf16[768,3072]{1,0:T(8,128)(2,1)S(1)}, u32[]{:S(2)}) copy-start(bf16[768,3072]{1,0:T(8,128)(2,1)S(1)} %get-tuple-element.105) | copy-start | bytes 14155780
  218.4 6.1 copy-start.6
  223.4 1.1 copy-start.16
  227.1 16.0 %slice-start = ((s8[4718592]{0:T(1024)(128)(4,1)}), s8[4194304]{0:T(1024)(128)(4,1)S(1)}, s32[]{:S(2)}) async-start(s8[4718592]{0:T(1024)(128)(4,1)} %bitcast.115), calls=%async_computation | async-start | bytes 8388608
  229.5 0.9 copy-start.24
  230.4 12.8 %copy-start.8 = (bf16[768,768]{1,0:T(8,128)(2,1)}, bf16[768,768]{1,0:T(8,128)(2,1)S(1)}, u32[]{:S(2)}) copy-start(bf16[768,768]{1,0:T(8,128)(2,1)S(1)} %get-tuple-element.96) | copy-start | bytes 3538948
  230.4 12.8 %copy-start.2 = (f32[768,768]{1,0:T(8,128)S(1)}, f32[768,768]{1,0:T(8,128)}, u32[]{:S(2)}) copy-start(f32[768,768]{1,0:T(8,128)} %copy-done.1) | copy-start | bytes 7077892
  230.4 12.8 %copy-start.18 = (f32[768]{0:T(1024)S(1)}, f32[768]{0:T(1024)}, u32[]{:S(2)}) copy-start(f32[768]{0:T(1024)} %copy-done.17) | copy-start | bytes 9220
  230.4 12.8 %copy-start.21 = (f32[768]{0:T(1024)S(1)}, f32[768]{0:T(1024)}, u32[]{:S(2)}) copy-start(f32[768]{0:T(1024)} %copy-done.20) | copy-start | bytes 9220
  230.4 12.8 %slice-start.1 = ((s8[4718592]{0:T(1024)(128)(4,1)}), s8[524288]{0:T(1024)(128)(4,1)S(1)}, s32[]{:S(2)}) async-start(s8[4718592]{0:T(1024)(128)(4,1)} %bitcast.115), calls=%async_computation.1 | async-start | bytes 1048576
  243.2 5.1 copy-start.28
  249.2 2.3 copy-start.27
  250.1 1.4 copy-start.4
  345.6 9.3 %copy-start = (bf16[3,192,3072]{2,1,0:T(8,128)(2,1)S(1)}, bf16[3,192,3072]{2,1,0:T(8,128)(2,1)}, u32[]{:S(2)}) copy-start(bf16[3,192,3072]{2,1,0:T(8,128)(2,1)} %shard_map.275) | copy-start | bytes 10616836
  464.2 5.2 copy-start.3
  464.2 5.2 copy-start.15
  464.2 5.2 copy-start.19
  464.2 5.2 copy-start.22
  464.2 5.2 copy-start.26
  469.4 8.6 %copy-start.9 = (bf16[768,768]{1,0:T(8,128)(2,1)S(1)}, bf16[768,768]{1,0:T(8,128)(2,1)}, u32[]{:S(2)}) copy-start(bf16[768,768]{1,0:T(8,128)(2,1)} %copy-done.8) | copy-start | bytes 3538948
  478.0 8.2 %copy-start.5 = (f32[768,768]{1,0:T(8,128)S(1)}, f32[768,768]{1,0:T(8,128)}, u32[]{:S(2)}) copy-start(f32[768,768]{1,0:T(8,128)} %copy-done.4) | copy-start | bytes 7077892
  478.0 8.2 %copy-start.10 = (bf16[768,768]{1,0:T(8,128)(2,1)S(1)}, bf16[768,768]{1,0:T(8,128)(2,1)}, u32[]{:S(2)}) copy-start(bf16[768,768]{1,0:T(8,128)(2,1)} %shard_map.273) | copy-start | bytes 3538948
  625.9 5.3 copy-start.12
  625.9 6.4 %copy-start.11 = (bf16[768,768]{1,0:T(8,128)(2,1)S(1)}, bf16[768,768]{1,0:T(8,128)(2,1)}, u32[]{:S(2)}) copy-start(bf16[768,768]{1,0:T(8,128)(2,1)} %get-tuple-element.42) | copy-start | bytes 3538948

commit v2 on v0

v2 whole, which is shorter than its diff:
```python
import functools
import math

import jax
import jax.numpy as jnp
from jax import lax
from jax.experimental import pallas as pl
from jax.experimental.pallas import tpu as pltpu
from jax.sharding import PartitionSpec as P

HEADS = 12
HD = 64
ROWS = 80
MESH = pl.DeviceIdType.MESH
f32 = jnp.float32
bf16 = jnp.bfloat16
epsilon = 1e-12
neg_large = -1e30
LOG2E = math.log2(math.e)
LN2 = math.log(2.0)
VMEM_LIMIT = 60 << 20

NN = (((1,), (0,)), ((), ()))
NT = (((1,), (1,)), ((), ()))
TN = (((0,), (0,)), ((), ()))


def mm(left, right, dims=NN):
    return lax.dot_general(left, right, dims, preferred_element_type=f32)


class Place:
    def __init__(self, n):
        self.n = n
        self.hi_n = 4 if n % 4 == 0 else 1
        self.lo_n = n // self.hi_n
        self.s = lax.axis_index("seq")
        self.i = lax.axis_index("shard")
        self.core = lax.rem(self.s, 2)
        self.mate = self.s + 1 - 2 * self.core
        self.far = lax.rem(self.s + 2, 4)
        self.hi = self.i // self.lo_n
        self.lo = lax.rem(self.i, self.lo_n)

    def at_hi(self, hi):
        return (self.s, hi * self.lo_n + self.lo)

    def at_lo(self, lo):
        return (self.s, self.hi * self.lo_n + lo)

    def on_seq(self, s):
        return (s, self.i)


def meet(peers):
    bar = pltpu.get_barrier_semaphore()
    for peer in peers:
        pl.semaphore_signal(bar, inc=1, device_id=peer, device_id_type=MESH)
    pl.semaphore_wait(bar, len(peers))


def rcopy(src, dst, send, recv, peer):
    return pltpu.make_async_remote_copy(
        src_ref=src, dst_ref=dst, send_sem=send, recv_sem=recv, device_id=peer, device_id_type=MESH
    )


def half(cols, core):
    return pl.ds(pl.multiple_of(core * (cols // 2), 128), cols // 2)


def gather_sems(n, count):
    dma = pltpu.SemaphoreType.DMA
    return [dma((count, 2 * n)), dma((count, n)), dma((count, n)), dma((count, n)), dma((count, 3 * n)), dma((count, 3 * n)), dma((count,))]


class Gather:
    def __init__(self, place, idx, src, dst, mode, sems):
        self.p, self.a, self.src, self.dst, self.mode = place, idx, src, dst, mode
        self.s1, self.r1, self.s2, self.r2, self.s3, self.r3, self.own = sems

    def view(self, ref, core, chip=None):
        cols = ref.shape[-1]
        if self.mode == "whole":
            return ref
        if self.mode == "half" or chip is None:
            return ref.at[:, half(cols, core)]
        at = core * (cols // 2) + chip * (cols // 4)
        return ref.at[:, pl.ds(pl.multiple_of(at, 128), cols // 4)]

    def mine(self, ref):
        return self.view(ref, self.p.core, self.p.s // 2)

    def local(self):
        return pltpu.make_async_copy(self.src, self.dst.at[self.p.i], self.own.at[self.a])

    def along_hi(self, hi, step):
        p, a = self.p, self.a
        blk = hi * p.lo_n + p.lo
        there = self.mine(self.dst.at[blk])
        return lambda own: rcopy(
            self.mine(self.src) if own else there, there, self.s1.at[a, blk if step > 0 else p.n + blk], self.r1.at[a, blk],
            p.at_hi(p.hi + step),
        )

    def along_lo(self, hi, j, own=False):
        p, a = self.p, self.a
        blk = hi * p.lo_n + p.lo
        there = self.mine(self.dst.at[blk])
        return rcopy(
            self.mine(self.src) if own else there, there, self.s2.at[a, hi * p.lo_n + j], self.r2.at[a, blk],
            p.at_lo(lax.rem(p.lo + j, p.lo_n)),
        )

    def to_far(self, blk, chip):
        p, a = self.p, self.a
        here = self.view(self.dst.at[blk], p.core, chip)
        return rcopy(here, here, self.s3.at[a, 2 * p.n + blk], self.r3.at[a, 2 * p.n + blk], p.on_seq(p.far))

    def to_mate(self, blk, core, chip=None):
        p, a = self.p, self.a
        here = self.view(self.dst.at[blk], core, chip)
        at = blk if chip is None else chip * p.n + blk
        return rcopy(here, here, self.s3.at[a, at], self.r3.at[a, at], p.on_seq(p.mate))

    def here(self, blk):
        if self.mode == "half":
            self.to_mate(blk, self.p.core).start()
        if self.mode == "quarter":
            self.to_far(blk, self.p.s // 2).start()
            self.to_mate(blk, self.p.core, self.p.s // 2).start()

    def start(self):
        p = self.p
        self.local().start()
        for step in (1, -1):

            @pl.when((p.hi + step >= 0) & (p.hi + step < p.hi_n))
            def _(step=step):
                self.along_hi(p.hi, step)(True).start()

        for j in range(1, p.lo_n):
            self.along_lo(p.hi, j, True).start()

    def come(self, m, step):
        p = self.p
        hi = p.hi - step * m

        @pl.when((hi >= 0) & (hi < p.hi_n))
        def _():
            blk = hi * p.lo_n + p.lo
            there = self.mine(self.dst.at[blk])
            rcopy(there, there, self.s1.at[self.a, 0], self.r1.at[self.a, blk], p.at_hi(p.hi)).wait_recv()

            @pl.when((p.hi + step >= 0) & (p.hi + step < p.hi_n))
            def _():
                self.along_hi(hi, step)(False).start()

            for j in range(1, p.lo_n):
                self.along_lo(hi, j).start()
            self.here(blk)

    def pass_on(self, m):
        self.come(m, 1)
        self.come(m, -1)

    def both_ways(self, m, body):
        p = self.p
        if m == 0:
            body(p.hi)
            return
        for step in (1, -1):
            hi = p.hi - step * m
            pl.when((hi >= 0) & (hi < p.hi_n))(lambda hi=hi: body(hi))

    def take_lo(self, m):
        p, a = self.p, self.a

        def body(hi):
            for j in range(1, p.lo_n):
                lo = lax.rem(p.lo + j, p.lo_n)
                blk = hi * p.lo_n + lo
                there = self.mine(self.dst.at[blk])
                rcopy(there, there, self.s2.at[a, 0], self.r2.at[a, blk], p.at_lo(lo)).wait_recv()
                self.here(blk)

        self.both_ways(m, body)

    def take_far(self, m):
        p = self.p

        def body(hi):
            for j in range(p.lo_n):
                if m or j:
                    blk = hi * p.lo_n + lax.rem(p.lo + j, p.lo_n)
                    self.to_far(blk, 1 - p.s // 2).wait_recv()
                    self.to_mate(blk, p.core, 1 - p.s // 2).start()

        if self.mode == "quarter":
            self.both_ways(m, body)

    def finish(self):
        p = self.p
        for m in range(p.hi_n):
            hi = lax.rem(p.hi + m, p.hi_n)
            for j in range(p.lo_n):
                blk = hi * p.lo_n + lax.rem(p.lo + j, p.lo_n)
                if self.mode != "whole" and (m or j):
                    for chip in (None,) if self.mode == "half" else (0, 1):
                        self.to_mate(blk, 1 - p.core, chip).wait_recv()
                        self.to_mate(blk, p.core, chip).wait_send()
                    if self.mode == "quarter":
                        self.to_far(blk, p.s // 2).wait_send()
                if j:
                    self.along_lo(hi, j).wait_send()
        for step in (1, -1):
            for m in range(p.hi_n):
                hi = p.hi - step * m

                @pl.when((hi >= 0) & (hi < p.hi_n) & (p.hi + step >= 0) & (p.hi + step < p.hi_n))
                def _(hi=hi, step=step):
                    self.along_hi(hi, step)(False).wait_send()

        self.local().wait()

    def steps(self):
        for m in range(1, self.p.hi_n):
            yield lambda m=m: self.pass_on(m)
        for m in range(self.p.hi_n):
            yield lambda m=m: self.take_lo(m)
        if self.mode == "quarter":
            for m in range(self.p.hi_n):
                yield lambda m=m: self.take_far(m)


def peers_of(p, seq_mates):
    out = [p.at_hi(lax.rem(p.hi + k, p.hi_n)) for k in range(1, p.hi_n)]
    out += [p.at_lo(lax.rem(p.lo + j, p.lo_n)) for j in range(1, p.lo_n)]
    return out + [p.on_seq(s) for s in seq_mates]


def gather_kernel(n, splits, chunks, *refs):
    count = len(splits)
    x_ref, srcs = refs[0], refs[1 : 1 + count]
    xg_ref, dsts = refs[1 + count], refs[2 + count : 2 + 2 * count]
    sems = refs[2 + 2 * count : 9 + 2 * count]
    xsem, xs1, xr1, xs2, xr2, xown = refs[9 + 2 * count :]
    p = Place(n)
    meet(peers_of(p, (p.mate, p.far)))
    rows = x_ref.shape[0] // chunks
    part = lambda q: pl.ds(q * rows, rows)
    sent = []
    for q in range(chunks):
        cp = rcopy(x_ref.at[part(q)], xg_ref.at[p.s, part(q)], xs1.at[q], xr1.at[q], p.on_seq(p.far))
        cp.start()
        sent.append(cp)
    gathers = [Gather(p, a, srcs[a], dsts[a], splits[a], sems) for a in range(count)]
    for g in gathers:
        g.start()
    own = pltpu.make_async_copy(x_ref, xg_ref.at[p.s], xown)
    own.start()
    cp = rcopy(x_ref, xg_ref.at[p.s], xsem.at[0], xsem.at[1], p.on_seq(p.mate))
    cp.start()
    sent.append(cp)
    for m in range(1, p.hi_n):
        for g in gathers:
            g.pass_on(m)
    for m in range(p.hi_n):
        for g in gathers:
            g.take_lo(m)
    for q in range(chunks):
        here = xg_ref.at[p.far, part(q)]
        rcopy(here, here, xs1.at[q], xr1.at[q], p.on_seq(p.far)).wait_recv()
        cp = rcopy(here, here, xs2.at[q], xr2.at[q], p.on_seq(p.mate))
        cp.start()
        sent.append(cp)
    there = xg_ref.at[p.mate]
    rcopy(there, there, xsem.at[0], xsem.at[1], p.on_seq(p.mate)).wait_recv()
    for q in range(chunks):
        there = xg_ref.at[3 - p.s, part(q)]
        rcopy(there, there, xs2.at[q], xr2.at[q], p.on_seq(p.mate)).wait_recv()
    for g in gathers:
        g.finish()
    for cp in sent:
        cp.wait_send()
    own.wait()


def gather_all(x, arrays, splits, n, cid):
    hi_n = 4 if n % 4 == 0 else 1
    chunks = 4
    count = len(arrays)
    anywhere = pl.BlockSpec(memory_space=pl.ANY)
    return pl.pallas_call(
        functools.partial(gather_kernel, n, splits, chunks),
        out_shape=[jax.ShapeDtypeStruct((4,) + x.shape, x.dtype)]
        + [jax.ShapeDtypeStruct((n,) + a.shape, a.dtype) for a in arrays],
        in_specs=[anywhere] * (1 + count),
        out_specs=[anywhere] * (1 + count),
        scratch_shapes=gather_sems(n, count)
        + [
            pltpu.SemaphoreType.DMA((2,)),
            pltpu.SemaphoreType.DMA((chunks,)),
            pltpu.SemaphoreType.DMA((chunks,)),
            pltpu.SemaphoreType.DMA((chunks,)),
            pltpu.SemaphoreType.DMA((chunks,)),
            pltpu.SemaphoreType.DMA,
        ],
        compiler_params=pltpu.CompilerParams(collective_id=cid, has_side_effects=True),
    )(x, *arrays)


CHUNK = 512
STOPS = (0, 1, 2, 3, 4, 5)


OFFSETS = (2, 1, 3, 0)
WHEN_HALF = {"lo": (1, 3, 5, 7), "owner": 14, "meet": 17}
WHEN_QUARTER = {"far": (3.1, 5.1, 6.1, 8.1), "lo": (5.2, 7.2, 8.2, 10.2), "owner": 15, "meet": 17}
WHEN_GATHER = ((1, 2, 3, 4, 6, 8, 10, 8, 9, 12, 15), (4, 8, 12, 5, 10, 14, 16))


def forward_kernel(n, heads, splits, x_ref, w_ref, b_ref, augq_ref, augk_ref, augv_ref, *refs):
    count = len(splits)
    srcs = refs[:count]
    q_ref, k_ref, v_ref, ctx_ref, lse_ref, wt_ref, merged_ref = refs[count : count + 7]
    dsts = refs[count + 7 : 2 * count + 7]
    sems = refs[2 * count + 7 : 2 * count + 14]
    xsend, xrecv, xown = refs[2 * count + 14 :]
    p = Place(n)
    h = pl.program_id(0)
    toks = x_ref.shape[0]
    part_toks = toks // 4
    gathers = [Gather(p, a, srcs[a], dsts[a], splits[a], sems) for a in range(count)]

    @pl.when(h == 0)
    def _():
        meet(peers_of(p, [lax.rem(p.s + k, 4) for k in range(1, 4)]))
        for g in gathers:
            g.start()
        wt_ref[...] = w_ref[...].T

    plan = [[] for _ in range(heads * len(STOPS))]
    for a, g in enumerate(gathers):
        for slot, step in zip(WHEN_GATHER[a], g.steps()):
            plan[slot].append(step)
    proj = mm(wt_ref[pl.ds(pl.multiple_of(h * 3 * HD, 64), 3 * HD)], x_ref[...], NT) + b_ref[0]
    scale = LOG2E / math.sqrt(HD)
    q_ref[0, :HD] = (proj[:HD] * scale).astype(bf16)
    q_ref[0, HD:] = augq_ref[...]
    k_ref[0, :HD] = proj[HD : 2 * HD].astype(bf16)
    k_ref[0, HD:] = augk_ref[...]
    v_ref[0, :HD] = proj[2 * HD :].astype(bf16)
    v_ref[0, HD:] = augv_ref[...]
    q = q_ref[0]
    top = jnp.full((1, toks), -3e38, f32)
    acc = jnp.zeros((ROWS, toks), f32)
    for j in range(toks // CHUNK):
        part = pl.ds(j * CHUNK, CHUNK)
        s = mm(k_ref[0, :, part], q, TN)
        new = jnp.maximum(top, jnp.max(s, axis=0, keepdims=True))
        probs = jnp.exp2(s - new).astype(bf16)
        acc = acc * jnp.exp2(top - new) + mm(v_ref[0, :, part], probs)
        top = new
        if j in STOPS:
            for hh in range(heads):
                steps = plan[hh * len(STOPS) + STOPS.index(j)]
                if steps:

                    @pl.when(h == hh)
                    def _(steps=steps):
                        for step in steps:
                            step()

    z = acc[HD : HD + 1]
    mine = pl.ds(pl.multiple_of(h * HD, HD), HD)
    ctx_ref[mine] = (acc[:HD] / z).astype(bf16)
    lse_ref[0] = jnp.broadcast_to(top + jnp.log2(z), (8, toks))

    def there(hh, src):
        return merged_ref.at[pl.ds(pl.multiple_of(src * heads * HD + hh * HD, HD), HD)]

    def out(hh, k):
        to = lax.rem(p.s + k, 4)
        block = ctx_ref.at[
            pl.ds(pl.multiple_of(hh * HD, HD), HD), pl.ds(pl.multiple_of(to * part_toks, 128), part_toks)
        ]
        if k == 0:
            return pltpu.make_async_copy(block, there(hh, p.s), xown.at[hh])
        return rcopy(block, there(hh, p.s), xsend.at[hh * 4 + k], xrecv.at[hh * 4 + p.s], p.on_seq(to))

    for k in (2, 3, 1, 0):
        out(h, k).start()

    @pl.when(h == heads - 1)
    def _():
        for g in gathers:
            g.finish()
        for hh in range(heads):
            for k in range(1, 4):
                frm = lax.rem(p.s + k, 4)
                rcopy(there(hh, frm), there(hh, frm), xsend.at[0], xrecv.at[hh * 4 + frm], p.on_seq(frm)).wait_recv()
                out(hh, k).wait_send()
            out(hh, 0).wait()


def attend(x, w, bias, augq, augk, augv, arrays, splits, n, cid):
    toks, width = x.shape
    cols = w.shape[1]
    heads = cols // (3 * HD)
    hi_n = 4 if n % 4 == 0 else 1
    count = len(arrays)
    one = pl.Buffered(1)
    fixed = lambda shape: pl.BlockSpec(shape, lambda h: (0, 0), pipeline_mode=one)
    anywhere = pl.BlockSpec(memory_space=pl.ANY)
    aug = fixed((ROWS - HD, toks))
    head = pl.BlockSpec((1, ROWS, toks), lambda h: (h, 0, 0))
    dma = pltpu.SemaphoreType.DMA
    return pl.pallas_call(
        functools.partial(forward_kernel, n, heads, splits),
        grid=(heads,),
        in_specs=[
            fixed(x.shape),
            fixed(w.shape),
            pl.BlockSpec((1, 3 * HD, 1), lambda h: (h, 0, 0)),
            aug,
            aug,
            aug,
        ]
        + [anywhere] * count,
        out_specs=[
            head,
            head,
            head,
            fixed((heads * HD, toks)),
            pl.BlockSpec((1, 8, toks), lambda h: (h, 0, 0)),
            fixed((cols, width)),
            anywhere,
        ]
        + [anywhere] * count,
        out_shape=[jax.ShapeDtypeStruct((heads, ROWS, toks), bf16)] * 3
        + [
            jax.ShapeDtypeStruct((heads * HD, toks), bf16),
            jax.ShapeDtypeStruct((heads, 8, toks), f32),
            jax.ShapeDtypeStruct((cols, width), bf16),
            jax.ShapeDtypeStruct((width, toks // 4), bf16),
        ]
        + [jax.ShapeDtypeStruct((n,) + a.shape, a.dtype) for a in arrays],
        scratch_shapes=gather_sems(n, count) + [dma((4 * heads,)), dma((4 * heads,)), dma((heads,))],
        compiler_params=pltpu.CompilerParams(collective_id=cid, has_side_effects=True, vmem_limit_bytes=VMEM_LIMIT),
    )(x, w, bias, augq, augk, augv, *arrays)


def three_parts(row):
    first = row.astype(bf16)
    rest = row - first.astype(f32)
    second = rest.astype(bf16)
    third = (rest - second.astype(f32)).astype(bf16)
    rows = lax.broadcasted_iota(jnp.int32, (8, row.shape[1]), 0)
    pick = lambda k, v: jnp.where(rows == k, jnp.broadcast_to(v.astype(f32), rows.shape), 0.0)
    return pick(0, first) + pick(1, second) + pick(2, third)


class VectorSum:
    def __init__(self, p, src, inbox, seqbox, sems):
        self.p, self.src, self.inbox, self.seqbox = p, src, inbox, seqbox
        self.vs, self.vr, self.ws, self.wr = sems

    @staticmethod
    def scratch(n, shape):
        dma = pltpu.SemaphoreType.DMA
        return [pltpu.VMEM((n,) + shape, f32), pltpu.VMEM((4,) + shape, f32), dma((n,)), dma((n,)), dma((4,)), dma((4,))]

    def to_shard(self, k):
        p = self.p
        return rcopy(self.src, self.inbox.at[p.i], self.vs.at[k], self.vr.at[p.i], (p.s, lax.rem(p.i + k, p.n)))

    def to_seq(self, k):
        p = self.p
        here = self.seqbox.at[p.s]
        return rcopy(here, here, self.ws.at[k], self.wr.at[p.s], p.on_seq(lax.rem(p.s + k, 4)))

    def start(self):
        for k in range(1, self.p.n):
            self.to_shard(k).start()
        self.inbox[self.p.i] = self.src[...]

    def over_seq(self):
        p = self.p
        for k in range(1, p.n):
            frm = lax.rem(p.i + k, p.n)
            there = self.inbox.at[frm]
            rcopy(there, there, self.vs.at[0], self.vr.at[frm], (p.s, frm)).wait_recv()
        self.seqbox[p.s] = jnp.sum(self.inbox[...], axis=0)
        for k in range(1, 4):
            self.to_seq(k).start()

    def finish(self):
        p = self.p
        for k in range(1, 4):
            frm = lax.rem(p.s + k, 4)
            there = self.seqbox.at[frm]
            rcopy(there, there, self.ws.at[0], self.wr.at[frm], p.on_seq(frm)).wait_recv()
            self.to_seq(k).wait_send()
        for k in range(1, p.n):
            self.to_shard(k).wait_send()


class Reduce:
    BUFS, SEMS = 5, 8

    def __init__(self, p, src, bufs, mode):
        self.p, self.src, self.mode = p, src, mode
        self.acc, self.side, self.inbox, self.far, self.out = bufs[:5]
        self.so, self.sh, self.rh, self.sl, self.rl, self.sx, self.rx, self.sf = bufs[5:]
        self.pieces = p.hi_n

    @staticmethod
    def scratch(n, hi_n, rows, w, mode):
        lo_n = n // hi_n
        dma = pltpu.SemaphoreType.DMA
        return [
            pltpu.VMEM((n, rows, w), bf16),
            pltpu.VMEM((lo_n, hi_n, rows, w), bf16),
            pltpu.VMEM((hi_n, rows, w), bf16),
            pltpu.VMEM((n if mode == "quarter" else 2, rows, w), bf16),
            pltpu.VMEM((2 if mode == "half" else 4, rows, w), bf16),
            dma((hi_n,)), dma((hi_n,)), dma((hi_n,)), dma((lo_n * hi_n,)), dma((lo_n * hi_n,)), dma((4,)), dma((4,)),
            dma((2 * hi_n,)),
        ]

    def hi_of(self, k):
        n = self.p.hi_n
        return lax.rem(self.p.hi + (OFFSETS[k] if n == 4 else k + 1), n)

    def blocks(self, ref, k):
        return ref.at[pl.ds(self.hi_of(k) * self.p.lo_n, self.p.lo_n)]

    def part(self, chip):
        return self.src.at[chip] if self.mode == "quarter" else self.src

    def load(self, k):
        src = self.part(self.p.s // 2)
        return pltpu.make_async_copy(self.blocks(src, k), self.blocks(self.acc, k), self.so.at[k])

    def swap_chips(self, k):
        p = self.p
        return rcopy(
            self.blocks(self.part(1 - p.s // 2), k), self.blocks(self.far, k), self.sf.at[k], self.sf.at[p.hi_n + k],
            p.on_seq(p.far),
        )

    def along_lo(self, k, j):
        p, d = self.p, self.hi_of(k)
        lo = lax.rem(p.lo + j, p.lo_n)
        src = self.acc if self.mode == "quarter" else self.src
        return rcopy(
            src.at[d * p.lo_n + lo], self.side.at[p.lo, d], self.sl.at[k * p.lo_n + j], self.rl.at[k * p.lo_n + p.lo],
            p.at_lo(lo),
        )

    def to_owner(self, k):
        p, d = self.p, self.hi_of(k)
        return rcopy(self.acc.at[d * p.lo_n + p.lo], self.inbox.at[p.hi], self.sh.at[k], self.rh.at[p.hi], p.at_hi(d))

    def start(self, k):
        if self.mode == "quarter":
            self.swap_chips(k).start()
        else:
            for j in range(1, self.p.lo_n):
                self.along_lo(k, j).start()
        self.load(k).start()

    def far_sum(self, k):
        if self.mode == "quarter":
            self.load(k).wait()
            self.swap_chips(k).wait_recv()
            here = self.blocks(self.acc, k)
            here[...] = (here[...].astype(f32) + self.blocks(self.far, k)[...].astype(f32)).astype(bf16)
            for j in range(1, self.p.lo_n):
                self.along_lo(k, j).start()

    def lo_sum(self, k):
        p, d = self.p, self.hi_of(k)
        if self.mode != "quarter":
            self.load(k).wait()
        mine = self.acc.at[d * p.lo_n + p.lo]
        total = mine[...].astype(f32)
        for j in range(1, p.lo_n):
            lo = lax.rem(p.lo + j, p.lo_n)
            there = self.side.at[lo, d]
            rcopy(there, there, self.sl.at[0], self.rl.at[k * p.lo_n + lo], p.at_lo(lo)).wait_recv()
            total = total + self.side[lo, d].astype(f32)
        mine[...] = total.astype(bf16)
        if k < self.pieces - 1:
            self.to_owner(k).start()

    def owner_sum(self):
        p = self.p
        total = self.acc[p.i].astype(f32)
        for k in range(self.pieces - 1):
            frm = self.hi_of(k)
            got = self.inbox.at[frm]
            rcopy(got, got, self.sh.at[0], self.rh.at[frm], p.at_hi(frm)).wait_recv()
            total = total + self.inbox[frm].astype(f32)
        if self.mode == "half":
            self.far[0] = total.astype(bf16)
            self.to_far().start()
        else:
            self.out[p.s] = total.astype(bf16)
            for k in (2, 3, 1):
                self.to_seq(k).start()

    def to_far(self):
        return rcopy(self.far.at[0], self.far.at[1], self.sx.at[0], self.rx.at[0], self.p.on_seq(self.p.far))

    def to_seq(self, k):
        p = self.p
        here = self.out.at[p.s]
        return rcopy(here, here, self.sx.at[k], self.rx.at[p.s], p.on_seq(lax.rem(p.s + k, 4)))

    def to_mate(self, core):
        here = self.out.at[core]
        return rcopy(here, here, self.sx.at[1], self.rx.at[1], self.p.on_seq(self.p.mate))

    def meet_far(self):
        if self.mode == "half":
            self.to_far().wait_recv()
            self.out[self.p.core] = (self.far[0].astype(f32) + self.far[1].astype(f32)).astype(bf16)
            self.to_mate(self.p.core).start()

    def take_all(self):
        p = self.p
        if self.mode == "half":
            self.to_mate(1 - p.core).wait_recv()
        else:
            for k in range(1, 4):
                frm = lax.rem(p.s + k, 4)
                there = self.out.at[frm]
                rcopy(there, there, self.sx.at[0], self.rx.at[frm], p.on_seq(frm)).wait_recv()

    def store(self, ref):
        w = self.out.shape[2]
        if self.mode == "half":
            for core in range(2):
                ref[:, core * w : (core + 1) * w] = self.out[core].astype(f32)
        else:
            for s in range(4):
                for c in range(w // 128):
                    at = c * 512 + (s % 2) * 256 + (s // 2) * 128
                    ref[:, at : at + 128] = self.out[s, :, c * 128 : (c + 1) * 128].astype(f32)

    def drain(self):
        p = self.p
        if self.mode == "half":
            self.to_mate(p.core).wait_send()
            self.to_far().wait_send()
        else:
            for k in range(1, 4):
                self.to_seq(k).wait_send()
        for k in range(self.pieces):
            if self.mode == "quarter":
                self.swap_chips(k).wait_send()
            for j in range(1, p.lo_n):
                self.along_lo(k, j).wait_send()
            if k < self.pieces - 1:
                self.to_owner(k).wait_send()

    def timed(self, table):
        for k in range(self.pieces):
            if self.mode == "quarter":
                yield table["far"][k % 4], lambda k=k: self.far_sum(k)
            yield table["lo"][k % 4], lambda k=k: self.lo_sum(k)
        yield table["owner"], self.owner_sum
        yield table["meet"], self.meet_far


def backward_kernel(n, heads, modes, q_ref, k_ref, v_ref, ctx_ref, lse_ref, gm_ref, vec_ref, *refs):
    count = len(modes)
    srcs, refs = refs[:count], refs[count:]
    out_ref, vsum_ref, sums, refs = refs[0], refs[1], refs[2 : 2 + count], refs[2 + count :]
    qa, da, dq, dctx, xsend, xrecv, xown = refs[:7]
    vbufs, refs = refs[7:13], refs[13:]
    each = Reduce.BUFS + Reduce.SEMS
    p = Place(n)
    h = pl.program_id(0)
    toks = q_ref.shape[2]
    part_toks = toks // 4
    vec = VectorSum(p, vec_ref, vbufs[0], vbufs[1], vbufs[2:])
    reds = [Reduce(p, srcs[a], refs[a * each : (a + 1) * each], modes[a]) for a in range(count)]

    def landing(hh, src):
        return dctx.at[pl.ds(pl.multiple_of(hh * HD, HD), HD), pl.ds(pl.multiple_of(src * part_toks, 128), part_toks)]

    def give(hh, k):
        to = lax.rem(p.s + k, 4)
        block = gm_ref.at[pl.ds(pl.multiple_of(to * heads * HD + hh * HD, HD), HD)]
        if k == 0:
            return pltpu.make_async_copy(block, landing(hh, p.s), xown.at[hh])
        return rcopy(block, landing(hh, p.s), xsend.at[hh * 4 + k], xrecv.at[hh * 4 + p.s], p.on_seq(to))

    @pl.when(h == 0)
    def _():
        meet([(p.s, lax.rem(p.i + k, n)) for k in range(1, n)] + [p.on_seq(lax.rem(p.s + k, 4)) for k in range(1, 4)])
        for hh in range(heads):
            for k in (2, 3, 1, 0):
                give(hh, k).start()
        for k in range(p.hi_n):
            for r in reds:
                r.start(k)
        vec.start()

    for k in range(1, 4):
        frm = lax.rem(p.s + k, 4)
        rcopy(landing(h, frm), landing(h, frm), xsend.at[0], xrecv.at[h * 4 + frm], p.on_seq(frm)).wait_recv()
    give(h, 0).wait()

    slots = heads * len(STOPS)
    plan = [[] for _ in range(slots)]
    for r in reds:
        for slot, step in r.timed(WHEN_QUARTER if r.mode == "quarter" else WHEN_HALF):
            plan[min(int(slot), slots - 1)].append((slot, step))
    plan = [[step for _, step in sorted(todo, key=lambda x: x[0])] for todo in plan]
    plan[slots // 2].append(vec.over_seq)

    qa[:HD] = q_ref[h, :HD]
    mask = q_ref[h, HD : HD + 8].astype(f32)
    zero = jnp.zeros((8, toks), f32)
    qa[HD:] = jnp.concatenate([mask, three_parts(-lse_ref[h, :1])], axis=0).astype(bf16)
    grad = dctx[pl.ds(pl.multiple_of(h * HD, HD), HD)]
    delta = jnp.sum(grad.astype(f32) * ctx_ref[pl.ds(pl.multiple_of(h * HD, HD), HD)].astype(f32), axis=0, keepdims=True)
    da[:HD] = grad
    da[HD:] = jnp.concatenate([three_parts(-delta), zero], axis=0).astype(bf16)
    q, do = qa[...], da[...]
    for j in range(toks // CHUNK):
        part = pl.ds(j * CHUNK, CHUNK)
        k = k_ref[h, :, part]
        probs = jnp.exp2(mm(k, q, TN))
        gprobs = mm(v_ref[h, :, part], do, TN)
        ds = (probs * gprobs).astype(bf16)
        probs = probs.astype(bf16)
        out_ref[h, 2 * HD :, part] = mm(do[:HD], probs, NT).astype(bf16)
        out_ref[h, HD : 2 * HD, part] = (mm(q[:HD], ds, NT) * LN2).astype(bf16)
        dq_part = mm(k[:HD], ds)
        dq[...] = dq_part if j == 0 else dq[...] + dq_part
        if j in STOPS:
            for hh in range(heads):
                todo = plan[hh * len(STOPS) + STOPS.index(j)]
                if todo:

                    @pl.when(h == hh)
                    def _(todo=todo):
                        for step in todo:
                            step()

    out_ref[h, :HD] = (dq[...] * (1.0 / math.sqrt(HD))).astype(bf16)

    @pl.when(h == heads - 1)
    def _():
        vec.finish()
        vbox = vec.seqbox
        vsum_ref[...] = (vbox[0] + vbox[1]) + (vbox[2] + vbox[3])
        for a, r in enumerate(reds):
            r.take_all()
            r.store(sums[a])
        for r in reds:
            r.drain()
        for hh in range(heads):
            for k in range(1, 4):
                give(hh, k).wait_send()


def attend_back(q, k, v, ctx, lse, gm, vec, arrays, modes, n, cid):
    heads, _, toks = q.shape
    hi_n = 4 if n % 4 == 0 else 1
    count = len(arrays)
    one = pl.Buffered(1)
    fixed = lambda shape: pl.BlockSpec(shape, lambda h: (0,) * len(shape), pipeline_mode=one)
    anywhere = pl.BlockSpec(memory_space=pl.ANY)
    dma = pltpu.SemaphoreType.DMA
    sums = [(a.shape[-2], a.shape[-1] * (4 if mode == "quarter" else 2)) for a, mode in zip(arrays, modes)]
    scratch = [
        pltpu.VMEM((ROWS, toks), bf16),
        pltpu.VMEM((ROWS, toks), bf16),
        pltpu.VMEM((HD, toks), f32),
        pltpu.VMEM((heads * HD, toks), bf16),
        dma((4 * heads,)), dma((4 * heads,)), dma((heads,)),
    ] + VectorSum.scratch(n, vec.shape)
    for a, mode in zip(arrays, modes):
        scratch += Reduce.scratch(n, hi_n, a.shape[-2], a.shape[-1], mode)
    return pl.pallas_call(
        functools.partial(backward_kernel, n, heads, modes),
        grid=(heads,),
        in_specs=[
            fixed(q.shape),
            fixed(k.shape),
            fixed(v.shape),
            fixed(ctx.shape),
            fixed(lse.shape),
            anywhere,
            fixed(vec.shape),
        ]
        + [anywhere] * count,
        out_specs=[fixed((heads, 3 * HD, toks)), fixed(vec.shape)]
        + [fixed(s) for s in sums],
        out_shape=[jax.ShapeDtypeStruct((heads, 3 * HD, toks), bf16), jax.ShapeDtypeStruct(vec.shape, f32)]
        + [jax.ShapeDtypeStruct(s, f32) for s in sums],
        scratch_shapes=scratch,
        compiler_params=pltpu.CompilerParams(collective_id=cid, has_side_effects=True, vmem_limit_bytes=VMEM_LIMIT),
    )(q, k, v, ctx, lse, gm, vec, *arrays)


def finish_kernel(
    n, d_ref, x_ref, wt_ref, resid_ref, out_ref, dw_ref, brow_ref, part, near, give, far, dw, brow, sems, *refs
):
    p = Place(n)
    vec = VectorSum(p, brow, refs[0], refs[1], refs[2:6])
    rows, cols = dw_ref.shape[0], wt_ref.shape[0]
    red = Reduce(p, dw, refs[6:], "whole")
    meet([(p.s, lax.rem(p.i + k, n)) for k in range(1, n)] + [p.on_seq(lax.rem(p.s + k, 4)) for k in range(1, 4)])
    toks = resid_ref.shape[0]
    beyond = lax.rem(p.mate + 2, 4)

    def token_part(s):
        return mm(d_ref[:, pl.ds(pl.multiple_of(s * toks, 128), toks)], wt_ref[...], TN)

    def to_mate(slot):
        return rcopy(part.at[slot], near.at[slot], sems.at[slot], sems.at[2 + slot], p.on_seq(p.mate))

    def to_far():
        return rcopy(give, far, sems.at[4], sems.at[5], p.on_seq(p.far))

    part[0] = token_part(beyond).astype(bf16)
    to_mate(0).start()
    grad = mm(d_ref[...], x_ref[...]).T.astype(bf16)
    dw[...] = grad.reshape(dw.shape)
    for k in range(red.pieces):
        red.start(k)
    mine = token_part(p.far)
    to_mate(0).wait_recv()
    give[...] = (mine + near[0].astype(f32)).astype(bf16)
    to_far().start()
    part[1] = token_part(p.mate).astype(bf16)
    to_mate(1).start()
    brow[...] = mm(jnp.ones((8, d_ref.shape[1]), bf16), d_ref[...], NT)
    vec.start()
    total = resid_ref[...] + token_part(p.s)
    for k in range(red.pieces):
        red.lo_sum(k)
    red.owner_sum()
    to_mate(1).wait_recv()
    total = total + near[1].astype(f32)
    vec.over_seq()
    to_far().wait_recv()
    out_ref[...] = (total + far[...].astype(f32)).astype(bf16)
    red.take_all()
    heads = cols // (3 * HD)
    width = 4 * heads * HD
    for s in range(4):
        blk = red.out[s].astype(f32)
        for h in range(heads):
            for w in range(3):
                at = w * width + (s * heads + h) * HD
                dw_ref[:, at : at + HD] = blk[:, (3 * h + w) * HD : (3 * h + w + 1) * HD]
    vec.finish()
    brow_ref[...] = vec.seqbox[:, 0]
    red.drain()
    to_mate(0).wait_send()
    to_mate(1).wait_send()
    to_far().wait_send()


def finish(d, x, w_t, resid, n, cid):
    toks, width = resid.shape
    cols = w_t.shape[0]
    rows = width // n
    hi_n = 4 if n % 4 == 0 else 1
    vm = pl.BlockSpec(memory_space=pltpu.VMEM)
    dma = pltpu.SemaphoreType.DMA
    return pl.pallas_call(
        functools.partial(finish_kernel, n),
        out_shape=[
            jax.ShapeDtypeStruct((toks, width), bf16),
            jax.ShapeDtypeStruct((rows, 4 * cols), f32),
            jax.ShapeDtypeStruct((4, cols), f32),
        ],
        in_specs=[vm] * 4,
        out_specs=[vm] * 3,
        scratch_shapes=[
            pltpu.VMEM((2, toks, width), bf16),
            pltpu.VMEM((2, toks, width), bf16),
            pltpu.VMEM((toks, width), bf16),
            pltpu.VMEM((toks, width), bf16),
            pltpu.VMEM((n, rows, cols), bf16),
            pltpu.VMEM((8, cols), f32),
            dma((6,)),
        ]
        + VectorSum.scratch(n, (8, cols))
        + Reduce.scratch(n, hi_n, rows, cols, "whole"),
        compiler_params=pltpu.CompilerParams(collective_id=cid, has_side_effects=True, vmem_limit_bytes=VMEM_LIMIT),
    )(d, x, w_t, resid)


def norm_parts(value):
    centred = value - jnp.mean(value, axis=-1, keepdims=True)
    inv = lax.rsqrt(jnp.mean(centred * centred, axis=-1, keepdims=True) + epsilon)
    return centred * inv, inv


def norm_back(grad_hat, hat, inv):
    mean_grad = jnp.mean(grad_hat, axis=-1, keepdims=True)
    mean_both = jnp.mean(grad_hat * hat, axis=-1, keepdims=True)
    return inv * (grad_hat - mean_grad - hat * mean_both)


def ffn_kernel(
    n, chunks, scale_ref, merged_ref, tok_ref, teach_ref, live_ref, wo_ref, vec_ref, bup_ref, up0_ref, up1_ref, down_ref,
    result_ref, resid_ref, gm_ref, dout_ref, dup_ref, ddown_ref, dvec_ref, dbup_ref,
    low, hat, inv, acc, grad_low, act, slope, down_own, down_got, up_got, out_own, out_got, send, recv,
):
    i = pl.program_id(0)
    p = Place(n)
    row = lambda k: vec_ref[k : k + 1]
    col_sum = lambda v: jnp.sum(v, axis=0, keepdims=True)
    c = jnp.where(i < chunks, i, 2 * chunks - 1 - i)

    def swap(own, got, at):
        return rcopy(own.at[:, half(own.shape[1], 1 - p.core)], got, send.at[at], recv.at[at], p.on_seq(p.mate))

    def swap_down(k):
        return swap(down_own.at[k], down_got.at[k], k)

    def swap_up(k):
        return swap(act.at[k], up_got.at[k], chunks + k)

    def swap_out():
        return swap(out_own, out_got, 2 * chunks)

    def total(own, got):
        return own[:, half(own.shape[1], p.core)].astype(f32) + got[...].astype(f32)

    def settle(k):
        swap_down(k).wait_recv()
        rows = down_own.shape[1]
        ddown_ref[pl.ds(pl.multiple_of(k * rows, 16), rows)] = total(down_own.at[k], down_got.at[k]).astype(bf16)
        swap_up(k).wait_recv()
        both = total(act.at[k], up_got.at[k]).astype(bf16)
        cols = both.shape[1] // 2
        for chip in range(2):
            dup_ref[chip, :, pl.ds(pl.multiple_of(k * cols, 128), cols)] = both[:, chip * cols : (chip + 1) * cols]

    @pl.when(i == 0)
    def _():
        meet([p.on_seq(p.mate)])
        branch = mm(merged_ref[...], wo_ref[...], TN) + row(0)
        h, r = norm_parts(tok_ref[...].astype(f32) + branch)
        hat[...] = h
        inv[...] = r
        normed = h * row(1) + row(2)
        low[...] = normed.astype(bf16)
        acc[...] = normed + row(3)

    def forward(up_ref):
        pre = mm(low[...], up_ref[...]) + bup_ref[pl.ds(c, 1)]
        cdf = 0.5 + 0.5 * lax.erf(pre * math.sqrt(0.5))
        pdf = jnp.exp(-0.5 * pre * pre) * (1.0 / math.sqrt(2.0 * math.pi))
        a = (pre * cdf).astype(bf16)
        act[c] = a
        slope[c] = cdf + pre * pdf
        acc[...] += mm(a, down_ref[...])

    def choose(body):
        pl.when(c < chunks // 2)(lambda: body(up0_ref))
        pl.when(c >= chunks // 2)(lambda: body(up1_ref))

    @pl.when(i < chunks)
    def _():
        choose(forward)

    @pl.when(i == chunks - 1)
    def _():
        h, r = norm_parts(acc[...])
        result = h * row(4) + row(5)
        result_ref[...] = result.astype(bf16)
        grad = (result - teach_ref[...].astype(f32)) * (live_ref[...] * scale_ref[0])
        two = norm_back(grad * row(4), h, r)
        g = two.astype(bf16)
        grad_low[...] = g
        acc[...] = two
        dvec_ref[...] = jnp.zeros_like(dvec_ref)
        dvec_ref[3:4] = col_sum(g.astype(f32))
        dvec_ref[4:5] = col_sum(grad * h)
        dvec_ref[5:6] = col_sum(grad)

    def backward(up_ref):
        g = grad_low[...]
        grad_pre = (mm(g, down_ref[...], NT) * slope[c]).astype(bf16)
        dbup_ref[pl.ds(c, 1)] = col_sum(grad_pre.astype(f32))
        down_own[c] = mm(act[c], g, TN).astype(bf16)
        swap_down(c).start()
        act[c] = mm(low[...], grad_pre, TN).astype(bf16)
        swap_up(c).start()
        acc[...] += mm(grad_pre, up_ref[...], NT)

    @pl.when(i >= chunks)
    def _():
        choose(backward)

    @pl.when(i > chunks)
    def _():
        settle(c + 1)

    @pl.when(i == 2 * chunks - 1)
    def _():
        grad = acc[...]
        h = hat[...]
        one = norm_back(grad * row(1), h, inv[...])
        resid_ref[...] = one
        g = one.astype(bf16)
        out_own[...] = mm(merged_ref[...], g).astype(bf16)
        swap_out().start()
        dvec_ref[0:1] = col_sum(g.astype(f32))
        dvec_ref[1:2] = col_sum(grad * h)
        dvec_ref[2:3] = col_sum(grad)
        gm_ref[...] = mm(wo_ref[...], g, NT).astype(bf16)
        settle(0)
        swap_out().wait_recv()
        dout_ref[...] = total(out_own, out_got).astype(bf16)
        swap_out().wait_send()
        for k in range(chunks):
            swap_down(k).wait_send()
            swap_up(k).wait_send()


def feed_forward(scale, merged, tokens, teacher, live, w_out, vec, b_up, w_up0, w_up1, w_down, n, cid):
    toks, width = tokens.shape
    hidden = w_down.shape[0]
    size = 512
    chunks = hidden // size
    one = pl.Buffered(1)
    fixed = lambda shape: pl.BlockSpec(shape, lambda i: (0,) * len(shape), pipeline_mode=one)
    turn = lambda i: jnp.where(i < chunks, i, 2 * chunks - 1 - i)
    dma = pltpu.SemaphoreType.DMA
    outs = [
        jax.ShapeDtypeStruct((toks, width), bf16),
        jax.ShapeDtypeStruct((toks, width), f32),
        jax.ShapeDtypeStruct(merged.shape, bf16),
        jax.ShapeDtypeStruct((width, width // 2), bf16),
        jax.ShapeDtypeStruct((2, width, hidden // 4), bf16),
        jax.ShapeDtypeStruct((hidden, width // 2), bf16),
        jax.ShapeDtypeStruct((8, width), f32),
        jax.ShapeDtypeStruct((chunks, size), f32),
    ]
    return pl.pallas_call(
        functools.partial(ffn_kernel, n, chunks),
        grid=(2 * chunks,),
        in_specs=[
            pl.BlockSpec(memory_space=pltpu.SMEM),
            fixed(merged.shape), fixed(tokens.shape), fixed(teacher.shape), fixed(live.shape), fixed(w_out.shape),
            fixed(vec.shape), fixed(b_up.shape),
            pl.BlockSpec((width, size), lambda i: (0, jnp.minimum(turn(i), chunks // 2 - 1))),
            pl.BlockSpec((width, size), lambda i: (0, jnp.maximum(turn(i) - chunks // 2, 0))),
            pl.BlockSpec((size, width), lambda i: (turn(i), 0)),
        ],
        out_specs=[fixed(o.shape) for o in outs],
        out_shape=outs,
        scratch_shapes=[
            pltpu.VMEM((toks, width), bf16),
            pltpu.VMEM((toks, width), f32),
            pltpu.VMEM((toks, 1), f32),
            pltpu.VMEM((toks, width), f32),
            pltpu.VMEM((toks, width), bf16),
            pltpu.VMEM((chunks, toks, size), bf16),
            pltpu.VMEM((chunks, toks, size), f32),
            pltpu.VMEM((chunks, size, width), bf16),
            pltpu.VMEM((chunks, size, width // 2), bf16),
            pltpu.VMEM((chunks, width, size // 2), bf16),
            pltpu.VMEM((width, width), bf16),
            pltpu.VMEM((width, width // 2), bf16),
            dma((2 * chunks + 1,)),
            dma((2 * chunks + 1,)),
        ],
        compiler_params=pltpu.CompilerParams(collective_id=cid, has_side_effects=True, vmem_limit_bytes=VMEM_LIMIT),
    )(scale, merged, tokens, teacher, live, w_out, vec, b_up, w_up0, w_up1, w_down)


def on_device(
    inputs, teacher, seq_lengths, w_qkv, q_bias, v_bias, w_out, out_bias, attn_gain, attn_shift, w_up, up_bias,
    w_down, down_bias, ffn_gain, ffn_shift,
):
    n = lax.axis_size("shard")
    s = lax.axis_index("seq")
    i = lax.axis_index("shard")
    toks, width = inputs.shape[1:]
    group = 4 * toks
    hidden = w_up.shape[1]
    rows = w_qkv.shape[0]
    heads = HEADS // 4
    folds = hidden // width
    tokens = inputs[0]
    lens = seq_lengths[0]
    ends = [lens[0], lens[0] + lens[1], lens[0] + lens[1] + lens[2]]

    own_w = lax.dynamic_index_in_dim(w_qkv.reshape(rows, 3, 4, heads, HD), s, 2, keepdims=False)
    own_w = jnp.transpose(own_w, (0, 2, 1, 3)).reshape(rows, heads * 3 * HD)
    live = jnp.stack([ends[2] // 64, lax.rem(ends[2], 64)]).astype(bf16)
    small = jnp.concatenate(
        [out_bias[None], attn_gain[None], attn_shift[None], down_bias[None], ffn_gain[None], ffn_shift[None], q_bias[None],
         v_bias[None], up_bias.reshape(folds, rows), jnp.broadcast_to(live[:, None], (2, rows))], axis=0
    )
    small = jnp.pad(small, ((0, 16 - small.shape[0]), (0, -rows % 128)))
    cut = hidden // 2
    xg, wq_g, small_g, wo_g, up0_g = gather_all(
        tokens, (own_w, small, w_out, w_up[:, :cut]), ("whole", "whole", "half", "half"), n, 1
    )
    x_all = xg.reshape(group, width)
    wq = wq_g.reshape(width, heads * 3 * HD)
    vecs = jnp.transpose(small_g[:, :, :rows], (1, 0, 2)).astype(f32)
    eight = vecs[:8].reshape(8, width)
    b_up = jnp.transpose(vecs[8 : 8 + folds], (1, 0, 2)).reshape(hidden // 512, 512)
    live_total = jnp.sum(vecs[8 + folds, :, 0]) * 64.0 + jnp.sum(vecs[9 + folds, :, 0])

    own_q, own_v = [
        lax.dynamic_slice_in_dim(eight[r], s * heads * HD, heads * HD).reshape(heads, 1, HD) for r in (6, 7)
    ]
    bias = jnp.concatenate([own_q, jnp.zeros_like(own_q), own_v], axis=1).reshape(heads, 3 * HD, 1)

    pos = lax.broadcasted_iota(jnp.int32, (16, group), 1)
    row = lax.broadcasted_iota(jnp.int32, (16, group), 0)
    seg = sum((pos >= e).astype(jnp.int32) for e in ends)
    augq = jnp.where((row < 4) & (seg != row), neg_large, 0.0).astype(bf16)
    augk = jnp.where((row < 4) & (seg == row) | (row >= 8) & (row < 11), 1.0, 0.0).astype(bf16)
    augv = jnp.where(row < 3, 1.0, 0.0).astype(bf16)

    q, k, v, ctx, lse, w_t, merged, up1_g, down_g = attend(
        x_all, wq, bias, augq, augk, augv, (w_up[:, cut:], w_down), ("quarter", "half"), n, 2
    )
    own_pos = s * toks + lax.iota(jnp.int32, toks)
    live_rows = (own_pos < ends[2]).astype(f32)[:, None]
    scale = (float(group * n) / live_total).reshape(1)
    result, grad_resid_one, gm, d_out, d_up, d_down, dvec, d_bup = feed_forward(
        scale, merged, tokens, teacher[0], live_rows, wo_g.reshape(width, width), eight, b_up,
        up0_g.reshape(width, cut), up1_g.reshape(width, cut),        down_g.reshape(hidden, width), n, 5,
    )
    vec = jnp.concatenate([dvec, d_bup.reshape(folds, width), jnp.zeros((8 - folds, width), f32)], axis=0)
    dqkv, vsum, d_up_r, d_down_r, d_out_r = attend_back(
        q, k, v, ctx, lse, gm, vec,
        (d_up.reshape(2, n, rows, hidden // 4), d_down.reshape(n, hidden // n, width // 2), d_out.reshape(n, rows, width // 2)),
        ("quarter", "half", "half"), n, 3,
    )
    grad_in, d_qkv, brow = finish(dqkv.reshape(heads * 3 * HD, group), x_all, w_t, grad_resid_one, n, 4)

    brow = jnp.transpose(brow.reshape(4, heads, 3, HD), (2, 0, 1, 3)).reshape(3, width)
    take = lambda v: lax.dynamic_slice_in_dim(v, i * rows, rows)
    vs = [take(vsum[r]) for r in range(6)]
    d_bup = lax.dynamic_slice_in_dim(vsum[8 : 8 + folds].reshape(hidden), i * (hidden // n), hidden // n)
    return (
        result[None], grad_in[None], d_qkv, take(brow[0]), take(brow[2]), d_out_r, vs[0], vs[1], vs[2], d_up_r, d_bup,
        d_down_r, vs[3], vs[4], vs[5],
    )


def solution(mesh):
    tokens, matrix, vector = P("shard", "seq", None), P("shard", None), P("shard")
    in_specs = (tokens, tokens, matrix, matrix, vector, vector, matrix, vector, vector, vector, matrix, vector, matrix,
                vector, vector, vector)
    out_specs = (tokens, tokens, matrix, vector, vector, matrix, vector, vector, vector, matrix, vector, matrix, vector,
                 vector, vector)
    return jax.shard_map(on_device, mesh=mesh, in_specs=in_specs, out_specs=out_specs, check_vma=False)
```

time: 1530 us -> 365 us (0.24); the launches traced: 1510 us -> 358 us
  waiting for transfers between devices: 515 us -> 0 us
  matrix products: 437 us -> 0 us
  Pallas kernels: 0 us -> 323 us
  local copies, waits for them, and re-layouts: 199 us -> 25.3 us
  blocking collectives: 173 us -> 0 us
  other arithmetic: 82.2 us -> 5.22 us
  loops' own time: 57.2 us -> 0 us
  starting transfers between devices: 25.2 us -> 0 us
    dot_general x138 -> x0, matrix products: 437 us -> none  [the longest x58 184 us: contract_cols(): lax.dot_general(left, right, (((1,), (1,)), ((), ())), preferred_element_...]
    reduce_scatter x3 -> x0, waiting for transfers between devices: 328 us -> none  [the longest x1 164 us: on_device(): lax.psum_scatter(grad_down, 'shard', scatter_dimension=0, tiled=True)]
    pallas_call x0 -> x5, Pallas kernels: none -> 323 us  [the longest x1 104 us: attend_back(): pl.pallas_call(functools.partial(backward_kernel, n, heads, modes), grid=...]
    unnamed x10 -> x0, waiting for transfers between devices: 107 us -> none
    all_to_all x1 -> x0, blocking collectives: 77.4 us -> none  [on_device(): lax.all_to_all(stacked[:, :, None, :], 'seq', split_axis=0, concat_axis=2...]
    dynamic_slice x102 -> x11, local copies, waits for them, and re-layouts: 67.8 us -> 5.47 us  [the longest x8 4.66 us: on_device(): take = lambda v: lax.dynamic_slice_in_dim(v, i * rows, rows)]
    another operation x5 -> x0, loops' own time: 57.2 us -> none  [the longest x1 35.8 us: on_device(): _, (ctx_blocks, lse_blocks) = lax.scan(attend, 0, flat_ids)]
    unnamed x2 -> x0, blocking collectives: 48.4 us -> none
  transfers between devices with their start and end apart: 12 -> 0, of which waited for: 6 -> 0; matrix products, arithmetic and copies ran while one was open for 43% -> 0% of each run, Pallas kernels for 0% -> 0%
where the time goes in v2:
time: 365 us; the launch traced here: 358 us
  Pallas kernels  323 us (88%)
  local copies, waits for them, and re-layouts  25.3 us (7%)
  other arithmetic  5.22 us (1%)
  between operations  4.35 us (1%)
    pallas_call x1, Pallas kernels, attend_back(): pl.pallas_call(functools.partial(backward_kernel, n, heads, modes), grid=...  104 us
    pallas_call x1, Pallas kernels, gather_all(): pl.pallas_call(functools.partial(gather_kernel, n, splits, chunks), out_s...  59.7 us
    pallas_call x1, Pallas kernels, attend(): pl.pallas_call(functools.partial(forward_kernel, n, heads, splits), grid=...  58.7 us
    pallas_call x1, Pallas kernels, finish(): pl.pallas_call(functools.partial(finish_kernel, n), out_shape=[jax.ShapeD...  51 us
    pallas_call x1, Pallas kernels, feed_forward(): pl.pallas_call(functools.partial(ffn_kernel, n, chunks), grid=(2 * chunks...  49.5 us
    unnamed x23, local copies, waits for them, and re-layouts  9.17 us

profile of v2, /device:TPU:15, one launch (start us, length us, event | category | flops | bytes accessed | tf_op | source)
XLA Modules:
  0.0 357.9 jit_solution(8012692050398612695)
XLA Ops:
  0.7 1.4 fusion.13
  4.1 0.8 reshape.151
  4.9 0.8 concatenate.14
  6.3 1.3 copy.42
  7.7 0.8 copy.44.refs_1_
  8.5 0.8 fusion.11
  9.3 59.7 %shard_map.271 = (bf16[4,768,768]{2,1,0:T(8,128)(2,1)}, bf16[8,96,576]{2,1,0:T(8,128)(2,1)}, bf16[8,16,128]{2,1,0:T(8,128)(2,1)}, bf16[8,96,768]{2,1,0:T(8,128)(2,1)}, bf16[8,96,1536]{2,1,0:T(8,128)(2,1)}) custom-call(bf16[768,768]{1,0:T(8,128)(2,1)} %bitcast.54, bf16[96,576]{1,0:T(8,128)(2,1)} %copy.44.refs_1_, bf16[16,128]{1,0:T(8,128)(2,1)} %pad.4.refs_2_, ...), custom_call_target="tpu_custom_call" | custom-call | tf_op jit(solution)/shard_map/pallas_call | solution.py:294
  69.1 0.8 convert_bitcast_fusion
  70.5 1.0 reshape.171.b_ref
  71.5 0.7 convert_add_fusion
  72.2 0.8 select_convert_fusion
  73.0 0.7 iota.48.augv_ref
  73.7 58.7 %shard_map.272 = (bf16[3,80,3072]{2,1,0:T(8,128)(2,1)}, bf16[3,80,3072]{2,1,0:T(8,128)(2,1)}, bf16[3,80,3072]{2,1,0:T(8,128)(2,1)}, bf16[192,3072]{1,0:T(8,128)(...) custom-call(bf16[3072,768]{1,0:T(8,128)(2,1)} %bitcast.52, ...), custom_call_target="tpu_custom_call" | custom-call | tf_op jit(solution)/shard_map/pallas_call | solution.py:419
  132.4 0.7 reshape.159.vec_ref
  133.1 0.7 reshape.160.bup_ref
  133.8 0.6 slice_reduce_fusion.4
  135.8 0.8 fusion.live_ref
  136.6 49.5 %shard_map.273 = (bf16[768,768]{1,0:T(8,128)(2,1)}, f32[768,768]{1,0:T(8,128)}, bf16[768,768]{1,0:T(8,128)(2,1)}, bf16[768,384]{1,0:T(8,128)(2,1)}, bf16[2,768,7...) custom-call(f32[1]{0:T(128)} %bitcast.19.scale_ref, ...), custom_call_target="tpu_custom_call" | custom-call | tf_op jit(solution)/shard_map/pallas_call | solution.py:1054
  186.0 0.7 reshape.164
  186.9 1.4 maximum_maximum_fusion.vec_ref
  188.3 104.1 %shard_map.274 = (bf16[3,192,3072]{2,1,0:T(8,128)(2,1)}, f32[16,768]{1,0:T(8,128)}, f32[96,3072]{1,0:T(8,128)}, f32[384,768]{1,0:T(8,128)}, f32[96,768]{1,0:T(8,128)}) custom-call(bf16[3,80,3072]{2,1,0:T(8,128)(2,1)} %get-tuple-element.54.q_ref, bf16[3,80,3072]{2,1,0:T(8,128)(2,1)} %get-tuple-element.55.k_ref, bf16[3,80,3072]{2,1,0:T(8,128)(2,1)} %get-tuple-element.56.v_ref, ...), custom_call_target="tpu_custom_call" | custom-call | tf_op jit(solution)/shard_map/pallas_call | solution.py:791
  292.4 51.0 %shard_map.275 = (bf16[768,768]{1,0:T(8,128)(2,1)}, f32[96,2304]{1,0:T(8,128)}, f32[4,576]{1,0:T(4,128)}) custom-call(bf16[576,3072]{1,0:T(8,128)(2,1)} %bitcast.57, bf16[3072,768]{1,0:T(8,128)(2,1)} %bitcast.53, bf16[576,768]{1,0:T(8,128)(2,1)} %get-tuple-element.66.wt_ref, f32[768,768]{1,0:T(8,128)} %get-tuple-element.67.resid_ref), custom_call_target="tpu_custom_call" | custom-call | tf_op jit(solution)/shard_map/pallas_call | solution.py:880
  343.4 0.8 reshape.169
  345.6 0.7 dynamic_slice.60
  349.8 1.0 copy.54
  350.8 0.7 copy-done.3
  351.5 1.0 copy.55
  353.1 0.9 copy.56
  354.2 0.7 copy.57
  354.9 1.0 copy.58
  355.9 0.7 copy-done.1
  356.6 1.0 copy.59
  (49 shorter events, 7.2 us)
Async XLA Ops:
  0.6 7.8 %copy-start.5 = (bf16[96,3072]{1,0:T(8,128)(2,1)S(1)}, bf16[96,3072]{1,0:T(8,128)(2,1)}, u32[]{:S(2)}) copy-start(bf16[96,3072]{1,0:T(8,128)(2,1)} %param.26) | copy-start | bytes 1769476
  292.3 53.2 %copy-start.7 = (f32[16,768]{1,0:T(8,128)S(1)}, f32[16,768]{1,0:T(8,128)}, u32[]{:S(2)}) copy-start(f32[16,768]{1,0:T(8,128)} %get-tuple-element.72) | copy-start | bytes 147460
  292.4 57.4 %copy-start = (bf16[768,768]{1,0:T(8,128)(2,1)S(1)}, bf16[768,768]{1,0:T(8,128)(2,1)}, u32[]{:S(2)}) copy-start(bf16[768,768]{1,0:T(8,128)(2,1)} %get-tuple-element.53) | copy-start | bytes 3538948
  349.8 1.7 copy-start.3
  351.5 1.6 copy-start.4
  353.1 1.1 copy-start.6
  353.1 1.8 copy-start.2
  354.9 1.7 copy-start.1
